TPU v7x, 1024 devices: a whole 4x8x16 slice. The times are simulated.
1024 devices in a mesh: seq: 64 (over z_hi, y, x), head: 16 (over z_lo, core).
Axes of the slice: x: 4, y: 8, z: 16 (z_hi: 2, z_lo: 8; z = z_hi * 8 + z_lo), core: 2. Of those that a mesh axis runs over, the one named last changes fastest.
Arguments:
- queries: bfloat16 [8192, 2048], P('seq', 'head'), may hold values from -108 to 108
- key_rows: bfloat16 [8192, 2048], P('seq', 'head'), may hold values from -4.5 to 4.5
- value_rows: bfloat16 [8192, 2048], P('seq', 'head'), may hold values from -6 to 6
- out_weight: bfloat16 [2048, 2048], P('head'), may hold values from -4 to 4
- strided_index: int32 [64, 8], P('seq'), may hold values from 0 to 15
- cotangent: bfloat16 [8192, 2048], P('seq'), may hold values from -6 to 6
Outputs:
- mixed_output: bfloat16 [8192, 2048], P('seq', 'head')
- grad_queries: bfloat16 [8192, 2048], P('seq', 'head')
- grad_keys: bfloat16 [8192, 2048], P('seq', 'head')
- grad_values: bfloat16 [8192, 2048], P('seq', 'head')
All inputs are finite; a program needn't handle non-finite values.
Results may differ from a plain program's by a relative error of at most 0.023.
Values may be sent and summed in bfloat16 or wider, within the bound.
A program may use at most 32 MiB of HBM per device.

v0:
```python
import jax
import jax.numpy as jnp
from jax import lax
from jax.sharding import PartitionSpec as P

HD = 128
BLK = 128
STRIDE_ROWS = 32


def padded(cells, sides, width):
    for axis, dim in sides:
        count = lax.axis_size(axis)
        head = lax.slice_in_dim(cells, 0, width, axis=dim)
        tail = lax.slice_in_dim(cells, cells.shape[dim] - width, cells.shape[dim], axis=dim)
        cells = jnp.concatenate(
            [
                lax.ppermute(tail, axis, [(i, (i + 1) % count) for i in range(count)]),
                cells,
                lax.ppermute(head, axis, [((i + 1) % count, i) for i in range(count)]),
            ],
            axis=dim,
        )
    return cells


def split_heads(array, head_size):
    return array.reshape(array.shape[:-1] + (array.shape[-1] // head_size, head_size))


def gather_lists(extended, strided_blocks, index_rows, group_size, block_rows):
    paired_width = extended.shape[1]
    window_rows = extended
    window_rows = window_rows.reshape(group_size + 2, block_rows, paired_width)
    window = jnp.stack([window_rows[:-2], window_rows[1:-1], window_rows[2:]], axis=1)
    picked = strided_blocks[index_rows]
    return jnp.concatenate([window, picked], axis=1).reshape(group_size, -1, paired_width)


def shards(queries, key_rows, value_rows, out_weight, strided_index, cotangent):
    tokens, feature_width = queries.shape
    block_rows = BLK
    per_device = tokens // block_rows
    group_size = min(per_device, max(1, 512 // block_rows))
    rounds = per_device // group_size
    score_scale = HD ** (-0.5)
    paired = jnp.concatenate([key_rows, value_rows], axis=1)
    extended = padded(paired, (("seq", 0),), block_rows)
    strided_local = lax.all_gather(paired[:STRIDE_ROWS], "seq", axis=0, tiled=True)
    side_count = strided_local.shape[0] // block_rows
    strided_blocks = strided_local.reshape(side_count, block_rows, 2 * feature_width)
    query_groups = queries.reshape(rounds, group_size, block_rows, feature_width)
    index_groups = strided_index.reshape(rounds, group_size, -1)
    numbers = jnp.arange(rounds, dtype=jnp.int32)

    def scores_for(query_group, key_list):
        query_heads = split_heads(query_group, HD)
        key_heads = split_heads(key_list[..., :feature_width], HD)
        return (
            jnp.einsum(
                "gqhd,gkhd->ghqk", query_heads, key_heads, preferred_element_type=jnp.float32
            )
            * score_scale
        )

    def forward(inputs):
        position, query_group, index_rows = inputs
        key_list = gather_lists(extended, strided_blocks, index_rows, group_size, block_rows)
        scores = scores_for(query_group, key_list)
        row_top = jnp.max(scores, axis=-1, keepdims=True)
        logsum = row_top + jnp.log(jnp.sum(jnp.exp(scores - row_top), axis=-1, keepdims=True))
        weights = jnp.exp(scores - logsum).astype(jnp.bfloat16)
        value_heads = split_heads(key_list[..., feature_width:], HD)
        output = jnp.einsum(
            "ghqk,gkhd->gqhd", weights, value_heads, preferred_element_type=jnp.float32
        )
        return (
            output.astype(jnp.bfloat16).reshape(group_size * block_rows, feature_width),
            logsum[..., 0],
        )

    attention_parts, logsums = lax.map(forward, (numbers, query_groups, index_groups))
    attention = attention_parts.reshape(tokens, feature_width)
    partial_terms = jnp.dot(attention, out_weight, preferred_element_type=jnp.float32)
    mixed_output = lax.psum_scatter(
        partial_terms.astype(jnp.bfloat16), "head", scatter_dimension=1, tiled=True
    )
    grad_attention = jnp.einsum(
        "td,fd->tf", cotangent, out_weight, preferred_element_type=jnp.float32
    ).astype(jnp.bfloat16)
    grad_groups = grad_attention.reshape(rounds, group_size, block_rows, feature_width)
    paired_width = 2 * feature_width
    side_numbers = jnp.arange(side_count, dtype=jnp.int32)

    def backward(state_pair, inputs):
        extended_sum, strided_sum = state_pair
        position, query_group, index_rows, grad_group, logsum = inputs
        key_list = gather_lists(extended, strided_blocks, index_rows, group_size, block_rows)
        scores = scores_for(query_group, key_list)
        probability = jnp.exp(scores - logsum[..., None])
        weights = probability.astype(jnp.bfloat16)
        query_heads = split_heads(query_group, HD)
        grad_heads = split_heads(grad_group, HD)
        key_heads = split_heads(key_list[..., :feature_width], HD)
        value_heads = split_heads(key_list[..., feature_width:], HD)
        grad_weights = jnp.einsum(
            "gqhd,gkhd->ghqk", grad_heads, value_heads, preferred_element_type=jnp.float32
        )
        row_delta = jnp.sum(probability * grad_weights, axis=-1, keepdims=True)
        grad_scores = (probability * (grad_weights - row_delta) * score_scale).astype(jnp.bfloat16)
        grad_query = jnp.einsum(
            "ghqk,gkhd->gqhd", grad_scores, key_heads, preferred_element_type=jnp.float32
        )
        grad_query = grad_query.astype(jnp.bfloat16).reshape(group_size * block_rows, feature_width)
        key_terms = jnp.einsum(
            "ghqk,gqhd->gkhd", grad_scores, query_heads, preferred_element_type=jnp.float32
        )
        value_terms = jnp.einsum(
            "ghqk,gqhd->gkhd", weights, grad_heads, preferred_element_type=jnp.float32
        )
        slot_terms = jnp.concatenate(
            [
                key_terms.reshape(group_size, -1, feature_width),
                value_terms.reshape(group_size, -1, feature_width),
            ],
            axis=2,
        )
        window = slot_terms[:, : 3 * block_rows].reshape(group_size, 3, block_rows, paired_width)
        window_sum = (
            jnp.pad(window[:, 0], ((0, 2), (0, 0), (0, 0)))
            + jnp.pad(window[:, 1], ((1, 1), (0, 0), (0, 0)))
            + jnp.pad(window[:, 2], ((2, 0), (0, 0), (0, 0)))
        )
        current = extended_sum
        extended_sum = current + window_sum.reshape(-1, paired_width)
        picked = slot_terms[:, 3 * block_rows :].reshape(-1, block_rows * paired_width)
        selector = (side_numbers[:, None] == index_rows).astype(jnp.float32)
        strided_sum = strided_sum + jnp.dot(
            selector, picked, precision=lax.Precision.HIGHEST, preferred_element_type=jnp.float32
        )
        return ((extended_sum, strided_sum), grad_query)

    start_state = (
        jnp.zeros((tokens + 2 * block_rows, paired_width), jnp.float32),
        jnp.zeros((side_count, block_rows * paired_width), jnp.float32),
    )
    final_state, grad_parts = lax.scan(
        backward, start_state, (numbers, query_groups, index_groups, grad_groups, logsums)
    )
    extended_sum, strided_sum = final_state
    rim_rows = jnp.concatenate([extended_sum[:block_rows], extended_sum[-block_rows:]], axis=0)
    returned = padded(rim_rows.astype(jnp.bfloat16), (("seq", 0),), block_rows).astype(
        rim_rows.dtype
    )
    own_grads = extended_sum[block_rows:-block_rows]
    own_grads = own_grads.at[:block_rows].add(returned[:block_rows])
    own_grads = own_grads.at[tokens - block_rows :].add(returned[3 * block_rows :])
    strided_mine = lax.psum_scatter(
        strided_sum.reshape(side_count * block_rows, paired_width),
        "seq",
        scatter_dimension=0,
        tiled=True,
    )
    own_grads = own_grads.at[: strided_mine.shape[0]].add(strided_mine)
    grad_queries = grad_parts.reshape(tokens, feature_width)
    grad_keys = own_grads[:, :feature_width].astype(jnp.bfloat16)
    grad_values = own_grads[:, feature_width:].astype(jnp.bfloat16)
    return (mixed_output, grad_queries, grad_keys, grad_values)


def solution(mesh):
    in_specs = (
        P("seq", "head"),
        P("seq", "head"),
        P("seq", "head"),
        P("head", None),
        P("seq", None),
        P("seq", None),
    )
    out_specs = (P("seq", "head"), P("seq", "head"), P("seq", "head"), P("seq", "head"))
    return jax.shard_map(shards, mesh=mesh, in_specs=in_specs, out_specs=out_specs, check_vma=False)
```

profile of v0, /device:TPU:64, one launch (start us, length us, event | category | flops | bytes accessed | tf_op | source)
XLA Modules:
  0.0 896.0 jit_solution(681169508522717535)
XLA Ops:
  7.2 0.8 constant_dynamic-update-slice_fusion.1
  8.0 0.8 constant_dynamic-update-slice_fusion
  9.5 23.6 %collective-permute-start.1 = (bf16[128,256]{1,0:T(8,128)(2,1)S(1)}, bf16[128,256]{1,0:T(8,128)(2,1)S(1)}, u32[]{:S(2)}, u32[]{:S(2)}) collective-permute-start(bf16[128,256]{1,0:T(8,128)(2,1)S(1)} %constant_dynamic-update-slice_fusion), channel_id=1, source_target_pairs={{16,0},{32,16},{48,32},{64,48},{80,64},{96,80},{112,96},{128,112},... | collective-permute-start | bytes 196616 | tf_op jit(solution)/shard_map/ppermute | solution.py:20
  33.1 1.9 collective-permute-start
  35.0 0.7 fusion.10
  35.7 1.3 convolution_convert_fusion.2
  37.0 145.9 %all-gather.2.cloned.1.call-done = bf16[2048,256]{1,0:T(8,128)(2,1)} async-done(((bf16[32,256]{1,0:T(8,128)(2,1)}), bf16[2048,256]{1,0:T(8,128)(2,1)}) %all-gather.2.cloned.1.call-update) | async-done | bytes 1048592 | tf_op jit(solution)/shard_map/all_gather | solution.py:49
  182.9 1.8 gather_fusion
  186.0 1.0 copy.27
  187.7 0.7 copy-done.5
  189.0 1.2 pad_maximum_fusion
  190.2 2.5 copy.24
  192.8 2.4 reshape.261
  195.2 2.2 fusion.8
  197.4 1.5 reshape.262
  198.9 1.1 copy-done.2
  200.3 3.5 collective-permute-start.2
  203.8 15.4 %collective-permute-start.3 = (bf16[128,256]{1,0:T(8,128)(2,1)S(1)}, bf16[128,256]{1,0:T(8,128)(2,1)S(1)}, u32[]{:S(2)}, u32[]{:S(2)}) collective-permute-start(bf16[128,256]{1,0:T(8,128)(2,1)S(1)} %get-tuple-element.128), channel_id=1, source_target_pairs={{16,0},{32,16},{48,32},{64,48},{80,64},{96,80},{112,96},{128,112},... | collective-permute-start | bytes 196616 | tf_op jit(solution)/shard_map/ppermute | solution.py:20
  219.5 0.7 copy.25
  220.3 0.9 collective-permute-done.3
  221.2 54.9 %reduce-scatter.7.cloned.1.call-done = bf16[128,128]{1,0:T(8,128)(2,1)} async-done(((bf16[2048,128]{1,0:T(8,128)(2,1)}), bf16[128,128]{1,0:T(8,128)(2,1)}) %reduce-scatter.7.cloned.1.call-update) | async-done | bytes 32784
  276.0 1.5 copy.28
  277.5 610.5 %reduce-scatter.5.cloned.1.call-done = f32[32,256]{1,0:T(8,128)} async-done(((f32[2048,256]{1,0:T(8,128)}), f32[32,256]{1,0:T(8,128)}) %reduce-scatter.5.cloned.1.call-update) | async-done | bytes 32784 | tf_op jit(solution)/shard_map/reduce_scatter | solution.py:158
  888.0 0.8 fusion.7
  (45 shorter events, 4.4 us)
Async XLA Ops:
  7.2 28.5 %copy-start = (bf16[128,2048]{1,0:T(8,128)(2,1)S(1)}, bf16[128,2048]{1,0:T(8,128)(2,1)}, u32[]{:S(2)}) copy-start(bf16[128,2048]{1,0:T(8,128)(2,1)} %param.19) | copy-start | bytes 1572868
  7.2 177.6 %copy-start.7 = (bf16[128,128]{1,0:T(8,128)(2,1)S(1)}, bf16[128,128]{1,0:T(8,128)(2,1)}, u32[]{:S(2)}) copy-start(bf16[128,128]{1,0:T(8,128)(2,1)} %param.16) | copy-start | bytes 98308
  7.2 175.7 %all-gather.2.cloned.1.call-start = ((), (), s32[]{:S(2)}) async-start(), calls=%async_computation.2 | async-start | bytes 1064960 | tf_op jit(solution)/shard_map/all_gather | solution.py:49
  9.4 266.6 %reduce-scatter.7.cloned.1.call-start = ((), (), s32[]{:S(2)}) async-start(), calls=%async_computation.4 | async-start | bytes 557056
  9.5 175.2 %collective-permute-start.1 = (bf16[128,256]{1,0:T(8,128)(2,1)S(1)}, bf16[128,256]{1,0:T(8,128)(2,1)S(1)}, u32[]{:S(2)}, u32[]{:S(2)}) collective-permute-start(bf16[128,256]{1,0:T(8,128)(2,1)S(1)} %constant_dynamic-update-slice_fusion), channel_id=1, source_target_pairs={{16,0},{32,16},{48,32},{64,48},{80,64},{96,80},{112,96},{128,112},... | collective-permute-start | bytes 196616 | tf_op jit(solution)/shard_map/ppermute | solution.py:20
  33.1 151.6 %collective-permute-start = (bf16[128,256]{1,0:T(8,128)(2,1)S(1)}, bf16[128,256]{1,0:T(8,128)(2,1)S(1)}, u32[]{:S(2)}, u32[]{:S(2)}) collective-permute-start(bf16[128,256]{1,0:T(8,128)(2,1)S(1)} %constant_dynamic-update-slice_fusion), channel_id=1, source_target_pairs={{0,16},{16,32},{32,48},{48,64},{64,80},{80,96},{96,112},{112,128},... | collective-permute-start | bytes 196616 | tf_op jit(solution)/shard_map/ppermute | solution.py:18
  184.8 2.3 copy-start.3
  187.0 701.0 %reduce-scatter.5.cloned.1.call-start = ((), (), s32[]{:S(2)}) async-start(), calls=%async_computation.3 | async-start | bytes 2129920 | tf_op jit(solution)/shard_map/reduce_scatter | solution.py:158
  187.6 0.7 copy-start.5
  189.0 3.8 copy-start.1
  190.2 5.0 copy-start.8
  198.9 1.1 copy-start.2
  200.0 19.2 %copy-start.4 = (bf16[1,11,128,256]{3,2,1,0:T(8,128)(2,1)S(1)}, bf16[1,11,128,256]{3,2,1,0:T(8,128)(2,1)}, u32[]{:S(2)}) copy-start(bf16[1,11,128,256]{3,2,1,0:T(8,128)(2,1)} %copy-done.3) | copy-start | bytes 2162692
  200.0 19.2 %copy-start.6 = (bf16[128,1408]{0,1:T(8,128)(2,1)S(1)}, bf16[128,1408]{0,1:T(8,128)(2,1)}, u32[]{:S(2)}) copy-start(bf16[128,1408]{0,1:T(8,128)(2,1)} %copy-done.5) | copy-start | bytes 1081348
  200.3 20.0 %collective-permute-start.2 = (bf16[128,256]{1,0:T(8,128)(2,1)S(1)}, bf16[128,256]{1,0:T(8,128)(2,1)S(1)}, u32[]{:S(2)}, u32[]{:S(2)}) collective-permute-start(bf16[128,256]{1,0:T(8,128)(2,1)S(1)} %get-tuple-element.127), channel_id=1, source_target_pairs={{0,16},{16,32},{32,48},{48,64},{64,80},{80,96},{96,112},{112,128},... | collective-permute-start | bytes 196616 | tf_op jit(solution)/shard_map/ppermute | solution.py:18
  203.8 17.3 %collective-permute-start.3 = (bf16[128,256]{1,0:T(8,128)(2,1)S(1)}, bf16[128,256]{1,0:T(8,128)(2,1)S(1)}, u32[]{:S(2)}, u32[]{:S(2)}) collective-permute-start(bf16[128,256]{1,0:T(8,128)(2,1)S(1)} %get-tuple-element.128), channel_id=1, source_target_pairs={{16,0},{32,16},{48,32},{64,48},{80,64},{96,80},{112,96},{128,112},... | collective-permute-start | bytes 196616 | tf_op jit(solution)/shard_map/ppermute | solution.py:20
Sparse Core Ops, SparseCore 0:
  14.4 168.4 all-gather.1
  187.2 88.8 reduce-scatter.6
  279.8 608.2 reduce-scatter.4
where the time goes:
time: 897 us; the launch traced here: 896 us
  waiting for transfers between devices  812 us (91%)
  starting transfers between devices  44.5 us (5%)
  local copies, waits for them, and re-layouts  16.3 us (2%)
  between operations  14 us (2%)
    reduce_scatter x1, waiting for transfers between devices, shards(): lax.psum_scatter(strided_sum.reshape(side_count * block_rows, paired_widt...  611 us
    all_gather x1, waiting for transfers between devices, shards(): lax.all_gather(paired[:STRIDE_ROWS], 'seq', axis=0, tiled=True)  146 us
    unnamed x4, waiting for transfers between devices  54.9 us
    ppermute x2, starting transfers between devices, padded(): lax.ppermute(head, axis, [((i + 1) % count, i) for i in range(count)])  38.9 us
  transfers between devices with their start and end apart: 7, of which 4 were waited for; matrix products, arithmetic and copies ran while one was open for 2% of the time, Pallas kernels for 0%

commit v1 on v0

v1 whole, which is shorter than its diff:
```python
import functools

import jax
import jax.numpy as jnp
from jax import lax
from jax.experimental import pallas as pl
from jax.experimental.pallas import tpu as pltpu
from jax.sharding import PartitionSpec as P

HD = 128
BLK = 128
ROWS = 32
GRID = (2, 8, 4)
GROUP = 4
MESH = pl.DeviceIdType.MESH
F32 = jnp.float32
BF16 = jnp.bfloat16
SCALE = HD ** -0.5
EXCLUDED = -1e30


def nt(a, b):
    return lax.dot_general(a, b, (((1,), (1,)), ((), ())), preferred_element_type=F32)


def nn(a, b):
    return lax.dot_general(a, b, (((1,), (0,)), ((), ())), preferred_element_type=F32)


def tn(a, b):
    return lax.dot_general(a, b, (((0,), (0,)), ((), ())), preferred_element_type=F32)


def kernel(
    dims, group, heads,
    q_hbm, k_hbm, v_hbm, w_hbm, index_ref, ct_hbm,
    mixed_ref, gq_ref, gk_ref, gv_ref,
    w_ref, ct_ref, win, kvg, qdo, bias, wg, stats, osend, orecv, attg, msend, mrecv,
    dqs, dqr, gws, gwr, gs, gy, gzs, gzr, s_ref, dw_ref,
    local_sem, w_local_sem,
    z_s, z_r, y_s, y_r, win_s, win_r, qdo_s, qdo_r, bias_s, bias_r, w_s, w_r,
    st_s, st_r, o_s, o_r, dq_s, dq_r, gw_s, gw_r, gy_s, gy_r, gz_s, gz_r, att_s, att_r, mix_s, mix_r,
):
    nz, ny, nx = dims
    count = nz * ny * nx
    groups = heads // group
    seq = lax.axis_index("seq")
    head = lax.axis_index("head")
    z, y, x = seq // (ny * nx), (seq // nx) % ny, seq % nx
    g, r = head // group, head % group

    def at(dz, dy, dx):
        return (((z + dz) % nz * ny + (y + dy) % ny) * nx + (x + dx) % nx, head)

    def member(d):
        return (seq, g * group + (r + d) % group)

    def other_group(e):
        return (seq, (g + e) % groups * group + r)

    following = ((seq + 1) % count, head)
    preceding = ((seq + count - 1) % count, head)

    def send(src, dst, send_sem, recv_sem, device):
        return pltpu.make_async_remote_copy(
            src_ref=src, dst_ref=dst, send_sem=send_sem, recv_sem=recv_sem,
            device_id=device, device_id_type=MESH,
        )

    started = []

    def start(src, dst, send_sem, recv_sem, device):
        copy = send(src, dst, send_sem, recv_sem, device)
        copy.start()
        started.append(copy)

    def received(dst, send_sem, recv_sem):
        send(dst, dst, send_sem, recv_sem, at(1, 0, 0)).wait_recv()

    loads = [
        pltpu.make_async_copy(k_hbm, win.at[1, 0], local_sem.at[0]),
        pltpu.make_async_copy(v_hbm, win.at[1, 1], local_sem.at[1]),
        pltpu.make_async_copy(q_hbm, qdo.at[0, 0], local_sem.at[2]),
        pltpu.make_async_copy(w_hbm, w_ref, local_sem.at[3]),
        pltpu.make_async_copy(ct_hbm, ct_ref, local_sem.at[4]),
    ]
    for load in loads:
        load.start()

    partners = [at(1, 0, 0)]
    partners += [at(0, d, 0) for d in range(1, ny)]
    partners += [at(0, 0, d) for d in range(1, nx)]
    partners += [following, preceding]
    partners += [member(d) for d in range(1, group)]
    partners += [other_group(e) for e in range(1, groups)]
    barrier = pltpu.get_barrier_semaphore()
    for device in partners:
        pl.semaphore_signal(barrier, inc=1, device_id=device, device_id_type=MESH)

    row = lax.broadcasted_iota(jnp.int32, (nz * ny, BLK), 0)
    block = ((z + row // ny) % nz * ny + (y + row % ny) % ny) * nx // (BLK // ROWS)
    listed = jnp.zeros((nz * ny, BLK), F32)
    for slot in range(index_ref.shape[1]):
        listed = listed + (block == index_ref[0, slot]).astype(F32)
    bias[0] = jnp.where(listed > 0, jnp.log(jnp.maximum(listed, 1.0)), EXCLUDED)

    loads[0].wait()
    loads[1].wait()
    kvg[0, 0] = win[1, :, :ROWS, :]
    pl.semaphore_wait(barrier, len(partners))

    start(kvg.at[0, 0], kvg.at[1, 0], z_s.at[0], z_r.at[0], at(1, 0, 0))
    for d in range(1, ny):
        start(kvg.at[0, 0], kvg.at[0, ny - d], y_s.at[0, d], y_r.at[0, d], at(0, d, 0))
    start(win.at[1], win.at[0], win_s.at[0], win_r.at[0], following)
    start(win.at[1], win.at[2], win_s.at[1], win_r.at[1], preceding)
    for d in range(1, nx):
        start(bias.at[0], bias.at[nx - d], bias_s.at[d], bias_r.at[d], at(0, 0, d))

    loads[2].wait()
    loads[3].wait()
    loads[4].wait()
    qdo[0, 1] = nt(ct_ref[...], w_ref[...]).astype(BF16)
    for d in range(1, nx):
        start(qdo.at[0], qdo.at[nx - d], qdo_s.at[d], qdo_r.at[d], at(0, 0, d))

    received(kvg.at[1, 0], z_s.at[0], z_r.at[0])
    for d in range(1, ny):
        start(kvg.at[1, 0], kvg.at[1, ny - d], y_s.at[1, d], y_r.at[1, d], at(0, d, 0))

    def columns(e, d):
        return pl.ds(pl.multiple_of(((g + e) % groups * group + (r + d) % group) * HD, HD), HD)

    w_loads = []
    for e in range(groups):
        to = pl.ds(e * HD, HD)
        load = pltpu.make_async_copy(w_hbm.at[:, columns(e, 0)], wg.at[0, :, to], w_local_sem.at[e])
        load.start()
        w_loads.append(load)
        for d in range(1, group):
            start(w_hbm.at[:, columns(e, d)], wg.at[group - d, :, to], w_s.at[d, e], w_r.at[d, e], member(d))

    received(win.at[0], win_s.at[0], win_r.at[0])
    received(win.at[2], win_s.at[1], win_r.at[1])
    key_w = win[:, 0].reshape(3 * BLK, HD)
    value_w = win[:, 1].reshape(3 * BLK, HD)
    query_own, grad_own = qdo[0, 0], qdo[0, 1]
    score_w = nt(key_w, query_own) * SCALE
    top_w = jnp.max(score_w, axis=0, keepdims=True)
    p_w = jnp.exp(score_w - top_w)
    sum_w = jnp.sum(p_w, axis=0, keepdims=True)
    dw_w = nt(value_w, grad_own)
    delta_w = jnp.sum(p_w * dw_w, axis=0, keepdims=True)
    o_w = tn(value_w, p_w.astype(BF16))

    for d in range(1, nx):
        received(bias.at[nx - d], bias_s.at[d], bias_r.at[d])
        received(qdo.at[nx - d], qdo_s.at[d], qdo_r.at[d])
    for plane in range(2):
        for d in range(1, ny):
            received(kvg.at[plane, ny - d], y_s.at[plane, d], y_r.at[plane, d])
    chunks = nz * ny
    keys = kvg[:, :, 0].reshape(chunks * ROWS, HD)
    values = kvg[:, :, 1].reshape(chunks * ROWS, HD)
    queries = qdo[:, 0].reshape(nx * BLK, HD)
    grads = qdo[:, 1].reshape(nx * BLK, HD)
    s_ref[...] = nt(keys, queries)
    dw_ref[...] = nt(values, grads)
    tops, sums, deltas = [], [], []
    for i in range(nx):
        lanes = pl.ds(i * BLK, BLK)
        spread = jnp.broadcast_to(bias[i][:, None, :], (chunks, ROWS, BLK)).reshape(chunks * ROWS, BLK)
        score = s_ref[:, lanes] * SCALE + spread
        top = jnp.max(score, axis=0, keepdims=True)
        p = jnp.exp(score - top)
        s_ref[:, lanes] = p
        tops.append(top)
        sums.append(jnp.sum(p, axis=0, keepdims=True))
        deltas.append(jnp.sum(p * dw_ref[:, lanes], axis=0, keepdims=True))
    for i in range(nx):
        top, total, delta = tops[i], sums[i], deltas[i]
        if i == 0:
            top = jnp.maximum(tops[0], top_w)
            a, b = jnp.exp(tops[0] - top), jnp.exp(top_w - top)
            total = a * sums[0] + b * sum_w
            delta = a * deltas[0] + b * delta_w
        stats[0, i, 0:1, :] = top
        stats[0, i, 1:2, :] = total
        stats[0, i, 2:3, :] = delta
        stats[0, i, 3:8, :] = jnp.zeros((5, BLK), F32)
    for d in range(1, nx):
        start(stats.at[0], stats.at[nx - d], st_s.at[d], st_r.at[d], at(0, 0, d))
    o_part = tn(values, s_ref[...].astype(BF16))
    for d in range(1, nx):
        osend[d] = o_part[:, d * BLK:(d + 1) * BLK].astype(BF16)
        start(osend.at[d], orecv.at[nx - d], o_s.at[d], o_r.at[d], at(0, 0, d))
    for d in range(1, nx):
        received(stats.at[nx - d], st_s.at[d], st_r.at[d])

    logsums, all_deltas = [], []
    for i in range(nx):
        entries = [(stats[p, (i - p) % nx, 0:1, :], stats[p, (i - p) % nx, 1:2, :], stats[p, (i - p) % nx, 2:3, :]) for p in range(nx)]
        top = functools.reduce(jnp.maximum, [e[0] for e in entries])
        logsum = top + jnp.log(sum(e[1] * jnp.exp(e[0] - top) for e in entries))
        logsums.append(logsum)
        all_deltas.append(sum(e[2] * jnp.exp(e[0] - logsum) for e in entries))

    factor_w = jnp.exp(top_w - logsums[0])
    attention = o_part[:, :BLK] * jnp.exp(tops[0] - logsums[0]) + o_w * factor_w
    for d in range(1, nx):
        p = nx - d
        received(orecv.at[p], o_s.at[d], o_r.at[d])
        attention = attention + orecv[p].astype(F32) * jnp.exp(stats[p, (-p) % nx, 0:1, :] - logsums[0])
    attg[0] = attention.astype(BF16)
    for d in range(1, group):
        start(attg.at[0], attg.at[group - d], att_s.at[d], att_r.at[d], member(d))

    weights, grad_scores = [], []
    for i in range(nx):
        lanes = pl.ds(i * BLK, BLK)
        probability = s_ref[:, lanes] * jnp.exp(tops[i] - logsums[i])
        weights.append(probability.astype(BF16))
        grad_scores.append((probability * (dw_ref[:, lanes] - all_deltas[i]) * SCALE).astype(BF16))
    weights = jnp.concatenate(weights, axis=1)
    grad_scores = jnp.concatenate(grad_scores, axis=1)
    gs[:, :, 0] = nn(grad_scores, queries).astype(BF16).reshape(nz, ny, ROWS, HD)
    gs[:, :, 1] = nn(weights, grads).astype(BF16).reshape(nz, ny, ROWS, HD)
    for plane in (1, 0):
        for d in range(1, ny):
            start(gs.at[plane, d], gy.at[plane, ny - d], gy_s.at[plane, d], gy_r.at[plane, d], at(0, d, 0))

    prob_w = p_w * factor_w
    ds_w = (prob_w * (dw_w - all_deltas[0]) * SCALE).astype(BF16)
    gk_w = nn(ds_w, query_own)
    gv_w = nn(prob_w.astype(BF16), grad_own)
    gws[0, 0] = gk_w[:BLK].astype(BF16)
    gws[0, 1] = gv_w[:BLK].astype(BF16)
    gws[1, 0] = gk_w[2 * BLK:].astype(BF16)
    gws[1, 1] = gv_w[2 * BLK:].astype(BF16)
    start(gws.at[0], gwr.at[0], gw_s.at[0], gw_r.at[0], preceding)
    start(gws.at[1], gwr.at[1], gw_s.at[1], gw_r.at[1], following)

    dq = tn(keys, grad_scores)
    for d in range(1, nx):
        dqs[d] = dq[:, d * BLK:(d + 1) * BLK].astype(BF16)
        start(dqs.at[d], dqr.at[nx - d], dq_s.at[d], dq_r.at[d], at(0, 0, d))
    dq_own = dq[:, :BLK] + tn(key_w, ds_w)

    for load in w_loads:
        load.wait()
    for d in range(1, group):
        for e in range(groups):
            received(wg.at[group - d, :, pl.ds(e * HD, HD)], w_s.at[d, e], w_r.at[d, e])
        received(attg.at[group - d], att_s.at[d], att_r.at[d])
    mixed = tn(attg[...].reshape(group * HD, BLK), wg[...].reshape(group * HD, groups * HD))
    for e in range(1, groups):
        msend[e] = mixed[:, e * HD:(e + 1) * HD].astype(BF16)
        start(msend.at[e], mrecv.at[groups - e], mix_s.at[e], mix_r.at[e], other_group(e))
    mixed_own = mixed[:, :HD]

    total = gs[1, 0].astype(F32)
    for d in range(1, ny):
        received(gy.at[1, ny - d], gy_s.at[1, d], gy_r.at[1, d])
        total = total + gy[1, ny - d].astype(F32)
    gzs[...] = total.astype(BF16)
    start(gzs, gzr, gz_s.at[0], gz_r.at[0], at(1, 0, 0))

    for d in range(1, nx):
        received(dqr.at[nx - d], dq_s.at[d], dq_r.at[d])
        dq_own = dq_own + dqr[nx - d].astype(F32)
    gq_ref[...] = dq_own.T.astype(BF16)

    received(gwr.at[0], gw_s.at[0], gw_r.at[0])
    received(gwr.at[1], gw_s.at[1], gw_r.at[1])
    own_k = gk_w[BLK:2 * BLK] + gwr[0, 0].astype(F32) + gwr[1, 0].astype(F32)
    own_v = gv_w[BLK:2 * BLK] + gwr[0, 1].astype(F32) + gwr[1, 1].astype(F32)
    gk_ref[ROWS:, :] = own_k[ROWS:].astype(BF16)
    gv_ref[ROWS:, :] = own_v[ROWS:].astype(BF16)

    total = gs[0, 0].astype(F32)
    for d in range(1, ny):
        received(gy.at[0, ny - d], gy_s.at[0, d], gy_r.at[0, d])
        total = total + gy[0, ny - d].astype(F32)

    for e in range(1, groups):
        received(mrecv.at[groups - e], mix_s.at[e], mix_r.at[e])
        mixed_own = mixed_own + mrecv[groups - e].astype(F32)
    mixed_ref[...] = mixed_own.astype(BF16)

    received(gzr, gz_s.at[0], gz_r.at[0])
    total = total + gzr[...].astype(F32)
    gk_ref[:ROWS, :] = (own_k[:ROWS] + total[0]).astype(BF16)
    gv_ref[:ROWS, :] = (own_v[:ROWS] + total[1]).astype(BF16)

    for copy in started:
        copy.wait_send()


def build(mesh, dims, group):
    nz, ny, nx = dims
    heads = mesh.shape["head"]
    groups = heads // group
    chunks = nz * ny

    def shards(queries, key_rows, value_rows, out_weight, strided_index, cotangent):
        width = out_weight.shape[1]
        dma = pltpu.SemaphoreType.DMA
        block = jax.ShapeDtypeStruct((BLK, HD), BF16)
        hbm = pl.BlockSpec(memory_space=pl.ANY)
        vmem = pl.BlockSpec(memory_space=pltpu.VMEM)
        square = lambda n: pltpu.VMEM((n, BLK, HD), BF16)
        pieces = lambda: pltpu.VMEM((nz, ny, 2, ROWS, HD), BF16)
        return pl.pallas_call(
            functools.partial(kernel, dims, group, heads),
            out_shape=(block,) * 4,
            in_specs=[hbm, hbm, hbm, hbm, pl.BlockSpec(memory_space=pltpu.SMEM), hbm],
            out_specs=(vmem,) * 4,
            scratch_shapes=[
                pltpu.VMEM((HD, width), BF16),
                pltpu.VMEM((BLK, width), BF16),
                pltpu.VMEM((3, 2, BLK, HD), BF16),
                pieces(),
                pltpu.VMEM((nx, 2, BLK, HD), BF16),
                pltpu.VMEM((nx, chunks, BLK), F32),
                pltpu.VMEM((group, HD, groups * HD), BF16),
                pltpu.VMEM((nx, nx, 8, BLK), F32),
                square(nx), square(nx),
                square(group),
                square(groups), square(groups),
                square(nx), square(nx),
                pltpu.VMEM((2, 2, BLK, HD), BF16), pltpu.VMEM((2, 2, BLK, HD), BF16),
                pieces(), pieces(),
                pltpu.VMEM((2, ROWS, HD), BF16), pltpu.VMEM((2, ROWS, HD), BF16),
                pltpu.VMEM((chunks * ROWS, nx * BLK), F32),
                pltpu.VMEM((chunks * ROWS, nx * BLK), F32),
                dma((5,)), dma((groups,)),
                dma((1,)), dma((1,)),
                dma((2, ny)), dma((2, ny)),
                dma((2,)), dma((2,)),
                dma((nx,)), dma((nx,)),
                dma((nx,)), dma((nx,)),
                dma((group, groups)), dma((group, groups)),
                dma((nx,)), dma((nx,)),
                dma((nx,)), dma((nx,)),
                dma((nx,)), dma((nx,)),
                dma((2,)), dma((2,)),
                dma((2, ny)), dma((2, ny)),
                dma((1,)), dma((1,)),
                dma((group,)), dma((group,)),
                dma((groups,)), dma((groups,)),
            ],
            compiler_params=pltpu.CompilerParams(
                collective_id=0, has_side_effects=True, vmem_limit_bytes=40 * 2 ** 20
            ),
        )(queries, key_rows, value_rows, out_weight, strided_index, cotangent)

    spread = P("seq", "head")
    return jax.shard_map(
        shards,
        mesh=mesh,
        in_specs=(spread, spread, spread, P("head", None), P("seq", None), P("seq", None)),
        out_specs=(spread,) * 4,
        check_vma=False,
    )


def solution(mesh):
    return build(mesh, GRID, GROUP)
```

time: 897 us -> 67.7 us (0.08)
  the two profiles are of different devices: /device:TPU:64 before, /device:TPU:1 now
where the time goes in v1:
time: 67.7 us; the launch traced here: 67.3 us
  Pallas kernels  59.1 us (87%)
  local copies, waits for them, and re-layouts  7.46 us (11%)
    pallas_call x1, Pallas kernels, shards(): pl.pallas_call(functools.partial(kernel, dims, group, heads), out_shape=(...  59.1 us
    unnamed x16, local copies, waits for them, and re-layouts  7.46 us

profile of v1, /device:TPU:1, one launch (start us, length us, event | category | flops | bytes accessed | tf_op | source)
XLA Modules:
  0.0 67.3 jit_solution(3790855097902103973)
XLA Ops:
  0.6 0.0 copy-start
  0.6 1.0 %copy-done = bf16[128,2048]{1,0:T(8,128)(2,1)S(1)} copy-done((bf16[128,2048]{1,0:T(8,128)(2,1)S(1)}, bf16[128,2048]{1,0:T(8,128)(2,1)}, u32[]{:S(2)}) %copy-start) | copy-done | bytes 524312
  1.7 0.0 copy-start.1
  1.7 1.0 %copy-done.1 = bf16[128,2048]{1,0:T(8,128)(2,1)S(1)} copy-done((bf16[128,2048]{1,0:T(8,128)(2,1)S(1)}, bf16[128,2048]{1,0:T(8,128)(2,1)}, u32[]{:S(2)}) %copy-start.1) | copy-done | bytes 524312
  2.7 0.0 copy-start.2
  2.7 0.8 %copy-done.2 = bf16[128,128]{1,0:T(8,128)(2,1)S(1)} copy-done((bf16[128,128]{1,0:T(8,128)(2,1)S(1)}, bf16[128,128]{1,0:T(8,128)(2,1)}, u32[]{:S(2)}) %copy-start.2) | copy-done | bytes 32792
  3.5 0.0 copy-start.3
  3.5 0.8 %copy-done.3 = bf16[128,128]{1,0:T(8,128)(2,1)S(1)} copy-done((bf16[128,128]{1,0:T(8,128)(2,1)S(1)}, bf16[128,128]{1,0:T(8,128)(2,1)}, u32[]{:S(2)}) %copy-start.3) | copy-done | bytes 32792
  4.2 0.0 copy-start.4
  4.2 0.8 %copy-done.4 = bf16[128,128]{1,0:T(8,128)(2,1)S(1)} copy-done((bf16[128,128]{1,0:T(8,128)(2,1)S(1)}, bf16[128,128]{1,0:T(8,128)(2,1)}, u32[]{:S(2)}) %copy-start.4) | copy-done | bytes 32792
  5.0 0.0 copy-start.5
  5.0 0.7 copy-done.5
  5.6 59.1 %shard_map.93 = (bf16[128,128]{1,0:T(8,128)(2,1)S(1)}, bf16[128,128]{1,0:T(8,128)(2,1)S(1)}, bf16[128,128]{1,0:T(8,128)(2,1)S(1)}, bf16[128,128]{1,0:T(8,128)(2,1)S(1)}) custom-call(bf16[128,128]{1,0:T(8,128)(2,1)S(1)} %copy-done.2, bf16[128,128]{1,0:T(8,128)(2,1)S(1)} %copy-done.3, bf16[128,128]{1,0:T(8,128)(2,1)S(1)} %copy-done.4, ...), custom_call_target="tpu_custom_call" | custom-call | tf_op jit(solution)/shard_map/pallas_call | solution.py:313
  64.8 0.6 copy.14
  65.4 0.6 copy.15
  66.0 0.6 copy.16
  66.6 0.6 copy.17
Async XLA Ops:
  0.6 1.0 %copy-start = (bf16[128,2048]{1,0:T(8,128)(2,1)S(1)}, bf16[128,2048]{1,0:T(8,128)(2,1)}, u32[]{:S(2)}) copy-start(bf16[128,2048]{1,0:T(8,128)(2,1)} %w_hbm.1) | copy-start | bytes 1572868
  1.7 1.0 %copy-start.1 = (bf16[128,2048]{1,0:T(8,128)(2,1)S(1)}, bf16[128,2048]{1,0:T(8,128)(2,1)}, u32[]{:S(2)}) copy-start(bf16[128,2048]{1,0:T(8,128)(2,1)} %ct_hbm.1) | copy-start | bytes 1572868
  2.7 0.8 %copy-start.2 = (bf16[128,128]{1,0:T(8,128)(2,1)S(1)}, bf16[128,128]{1,0:T(8,128)(2,1)}, u32[]{:S(2)}) copy-start(bf16[128,128]{1,0:T(8,128)(2,1)} %q_hbm.1) | copy-start | bytes 98308
  3.5 0.8 %copy-start.3 = (bf16[128,128]{1,0:T(8,128)(2,1)S(1)}, bf16[128,128]{1,0:T(8,128)(2,1)}, u32[]{:S(2)}) copy-start(bf16[128,128]{1,0:T(8,128)(2,1)} %k_hbm.1) | copy-start | bytes 98308
  4.2 0.8 %copy-start.4 = (bf16[128,128]{1,0:T(8,128)(2,1)S(1)}, bf16[128,128]{1,0:T(8,128)(2,1)}, u32[]{:S(2)}) copy-start(bf16[128,128]{1,0:T(8,128)(2,1)} %v_hbm.1) | copy-start | bytes 98308
  5.0 0.7 copy-start.5

commit v2 on v1

v2 whole, which is shorter than its diff:
```python
import functools

import jax
import jax.numpy as jnp
from jax import lax
from jax.experimental import pallas as pl
from jax.experimental.pallas import tpu as pltpu
from jax.sharding import PartitionSpec as P

HD = 128
BLK = 128
ROWS = 32
GRID = (2, 8, 4)
GROUP = 4
MESH = pl.DeviceIdType.MESH
F32 = jnp.float32
BF16 = jnp.bfloat16
SCALE = HD ** -0.5
EXCLUDED = -1e30


def nt(a, b):
    return lax.dot_general(a, b, (((1,), (1,)), ((), ())), preferred_element_type=F32)


def nn(a, b):
    return lax.dot_general(a, b, (((1,), (0,)), ((), ())), preferred_element_type=F32)


def tn(a, b):
    return lax.dot_general(a, b, (((0,), (0,)), ((), ())), preferred_element_type=F32)


def kernel(
    dims, group, heads,
    q_hbm, k_hbm, v_hbm, w_hbm, index_ref, ct_hbm,
    out_ref,
    w_ref, ct_ref, win, kvg, qdo, bias, wg, stats, osend, orecv, attg, msend, mrecv,
    dqs, dqr, gws, gwr, gs, gy, gzs, gzr, s_ref, dw_ref, seam_a, seam_b,
    local_sem, w_local_sem,
    z_s, z_r, y_s, y_r, win_s, win_r, out_s, in_r, over_s, over_r, last_s, qdo_s, qdo_r, bias_s, bias_r, w_s, w_r,
    st_s, st_r, o_s, o_r, dq_s, dq_r, gy_s, gy_r, gz_s, gz_r, att_s, att_r, mix_s, mix_r,
):
    nz, ny, nx = dims
    count = nz * ny * nx
    groups = heads // group
    seq = lax.axis_index("seq")
    head = lax.axis_index("head")
    z, y, x = seq // (ny * nx), (seq // nx) % ny, seq % nx
    g, r = head // group, head % group

    def at(dz, dy, dx):
        return (((z + dz) % nz * ny + (y + dy) % ny) * nx + (x + dx) % nx, head)

    def member(d):
        return (seq, g * group + (r + d) % group)

    def other_group(e):
        return (seq, (g + e) % groups * group + r)

    following = ((seq + 1) % count, head)
    preceding = ((seq + count - 1) % count, head)

    def send(src, dst, send_sem, recv_sem, device):
        return pltpu.make_async_remote_copy(
            src_ref=src, dst_ref=dst, send_sem=send_sem, recv_sem=recv_sem,
            device_id=device, device_id_type=MESH,
        )

    started, waited = {}, set()

    def start(name, src, dst, send_sem, recv_sem, device):
        copy = send(src, dst, send_sem, recv_sem, device)
        copy.start()
        started[name] = copy

    def received(*name):
        started[name].wait_recv()
        waited.add(name)

    piece = BLK // ny
    is_first = (y == 0) & (x == 0)
    is_last = (y == ny - 1) & (x == nx - 1)
    crossings = (
        (is_last, x == nx - 1, (y + 1) % ny, following, at(0, -y, 1)),
        (is_first, x == 0, y, preceding, at(0, ny - 1 - y, nx - 1)),
    )

    def seam_copy(kind, way, step, t, src, dst, device):
        semaphores = (
            (out_s.at[kind, way, t], in_r.at[kind, way]),
            (over_s.at[kind, way], over_r.at[kind, way]),
            (last_s.at[kind, way], win_r.at[kind, way]),
        )[step]
        return send(src, dst, *semaphores, device)

    def whole(kind, way, src, dst):
        return send(src, dst, win_s.at[kind, way], win_r.at[kind, way], crossings[way][3])

    def scattered(kind, way, src):
        return [
            seam_copy(kind, way, 0, t, src.at[:, t * piece:(t + 1) * piece], seam_a.at[kind, way], at(0, t, 0))
            for t in range(1, ny)
        ]

    def over(kind, way):
        return seam_copy(kind, way, 1, 0, seam_a.at[kind, way], seam_b.at[kind, way], at(1, 0, 0))

    def landing(kind, way, dst):
        rows = pl.ds(pl.multiple_of(crossings[way][2] * piece, piece), piece)
        return seam_copy(kind, way, 2, 0, seam_b.at[kind, way], dst.at[:, rows], crossings[way][4])

    def seam_send(kind, ends):
        for way, (src, dst) in enumerate(ends):
            source = crossings[way][0]

            @pl.when(source)
            def _():
                for copy in scattered(kind, way, src):
                    copy.start()
                seam_a[kind, way] = src[:, :piece]

            @pl.when(jnp.logical_not(source))
            def _():
                whole(kind, way, src, dst).start()

    def seam_over(kind, ends):
        for way in range(2):
            source, column = crossings[way][:2]

            @pl.when(column & jnp.logical_not(source))
            def _():
                scattered(kind, way, ends[way][0])[0].wait_recv()

            @pl.when(column)
            def _():
                over(kind, way).start()

    def seam_land(kind, ends):
        for way in range(2):
            @pl.when(crossings[way][1])
            def _():
                over(kind, way).wait_recv()
                landing(kind, way, ends[way][1]).start()

    def seam_received(kind, ends):
        for way, (src, dst) in enumerate(ends):
            whole(kind, way, src, dst).wait_recv()

    def seam_sent(kind, ends):
        for way, (src, dst) in enumerate(ends):
            source, column = crossings[way][:2]

            @pl.when(source)
            def _():
                for copy in scattered(kind, way, src):
                    copy.wait_send()

            @pl.when(jnp.logical_not(source))
            def _():
                whole(kind, way, src, dst).wait_send()

            @pl.when(column)
            def _():
                over(kind, way).wait_send()
                landing(kind, way, dst).wait_send()

    window_ends = ((win.at[1], win.at[0]), (win.at[1], win.at[2]))
    grad_ends = ((gws.at[1], gwr.at[1]), (gws.at[0], gwr.at[0]))

    partners = [at(1, 0, 0)]
    partners += [at(0, d, 0) for d in range(1, ny)]
    partners += [at(0, 0, d) for d in range(1, nx)]
    partners += [member(d) for d in range(1, group)]
    partners += [other_group(e) for e in range(1, groups)]
    barrier = pltpu.get_barrier_semaphore()

    def greet(device):
        pl.semaphore_signal(barrier, inc=1, device_id=device, device_id_type=MESH)

    for device in partners:
        greet(device)
    for way in range(2):
        @pl.when(jnp.logical_not(crossings[way][0]))
        def _():
            greet(crossings[way][3])

        @pl.when(crossings[1 - way][0])
        def _():
            for t in range(ny):
                greet(at(0, t, 1 if way else nx - 1))

    met = len(partners) + sum(
        jnp.logical_not(source).astype(jnp.int32) + column.astype(jnp.int32)
        for source, column in (c[:2] for c in crossings)
    )

    loads = [
        pltpu.make_async_copy(k_hbm, win.at[1, 0], local_sem.at[0]),
        pltpu.make_async_copy(v_hbm, win.at[1, 1], local_sem.at[1]),
        pltpu.make_async_copy(q_hbm, qdo.at[0, 0], local_sem.at[2]),
        pltpu.make_async_copy(w_hbm, w_ref, local_sem.at[3]),
        pltpu.make_async_copy(ct_hbm, ct_ref, local_sem.at[4]),
    ]
    for load in loads:
        load.start()

    row = lax.broadcasted_iota(jnp.int32, (nz * ny, BLK), 0)
    block = ((z + row // ny) % nz * ny + (y + row % ny) % ny) * nx // (BLK // ROWS)
    listed = jnp.zeros((nz * ny, BLK), F32)
    for slot in range(index_ref.shape[1]):
        listed = listed + (block == index_ref[0, slot]).astype(F32)
    bias[0] = jnp.where(listed > 0, jnp.log(jnp.maximum(listed, 1.0)), EXCLUDED)

    loads[0].wait()
    loads[1].wait()
    kvg[0, 0] = win[1, :, :ROWS, :]
    pl.semaphore_wait(barrier, met)

    start(("z", 0), kvg.at[0, 0], kvg.at[1, 0], z_s.at[0], z_r.at[0], at(1, 0, 0))
    for d in range(1, ny):
        start(("y", 0, d), kvg.at[0, 0], kvg.at[0, ny - d], y_s.at[0, d], y_r.at[0, d], at(0, d, 0))
    seam_send(0, window_ends)
    for d in range(1, nx):
        start(("bias", d), bias.at[0], bias.at[nx - d], bias_s.at[d], bias_r.at[d], at(0, 0, d))

    loads[2].wait()
    loads[3].wait()
    loads[4].wait()
    qdo[0, 1] = nt(ct_ref[...], w_ref[...]).astype(BF16)
    for d in range(1, nx):
        start(("qdo", d), qdo.at[0], qdo.at[nx - d], qdo_s.at[d], qdo_r.at[d], at(0, 0, d))

    received("z", 0)
    for d in range(1, ny):
        start(("y", 1, d), kvg.at[1, 0], kvg.at[1, ny - d], y_s.at[1, d], y_r.at[1, d], at(0, d, 0))

    seam_over(0, window_ends)
    def columns(e, d):
        return pl.ds(pl.multiple_of(((g + e) % groups * group + (r + d) % group) * HD, HD), HD)

    w_loads = []
    for e in range(groups):
        to = pl.ds(e * HD, HD)
        load = pltpu.make_async_copy(w_hbm.at[:, columns(e, 0)], wg.at[0, :, to], w_local_sem.at[e])
        load.start()
        w_loads.append(load)
        for d in range(1, group):
            start(("w", d, e), w_hbm.at[:, columns(e, d)], wg.at[group - d, :, to], w_s.at[d, e], w_r.at[d, e], member(d))

    for d in range(1, nx):
        received("bias", d)
        received("qdo", d)
    queries = qdo[:, 0].reshape(nx * BLK, HD)
    grads = qdo[:, 1].reshape(nx * BLK, HD)
    half = ny * ROWS

    def strided(plane):
        for d in range(1, ny):
            received("y", plane, d)
        rows = pl.ds(plane * half, half)
        keys = kvg[plane, :, 0].reshape(half, HD)
        values = kvg[plane, :, 1].reshape(half, HD)
        s_ref[rows, :] = nt(keys, queries)
        dw_ref[rows, :] = nt(values, grads)

    strided(0)

    seam_land(0, window_ends)
    seam_received(0, window_ends)
    key_w = win[:, 0].reshape(3 * BLK, HD)
    value_w = win[:, 1].reshape(3 * BLK, HD)
    query_own, grad_own = qdo[0, 0], qdo[0, 1]
    score_w = nt(key_w, query_own) * SCALE
    top_w = jnp.max(score_w, axis=0, keepdims=True)
    p_w = jnp.exp(score_w - top_w)
    sum_w = jnp.sum(p_w, axis=0, keepdims=True)
    dw_w = nt(value_w, grad_own)
    delta_w = jnp.sum(p_w * dw_w, axis=0, keepdims=True)
    o_w = tn(value_w, p_w.astype(BF16))

    strided(1)
    chunks = nz * ny
    keys = kvg[:, :, 0].reshape(chunks * ROWS, HD)
    values = kvg[:, :, 1].reshape(chunks * ROWS, HD)
    tops, sums, deltas = [], [], []
    for i in range(nx):
        lanes = pl.ds(i * BLK, BLK)
        spread = jnp.broadcast_to(bias[i][:, None, :], (chunks, ROWS, BLK)).reshape(chunks * ROWS, BLK)
        score = s_ref[:, lanes] * SCALE + spread
        top = jnp.max(score, axis=0, keepdims=True)
        p = jnp.exp(score - top)
        s_ref[:, lanes] = p
        tops.append(top)
        sums.append(jnp.sum(p, axis=0, keepdims=True))
        deltas.append(jnp.sum(p * dw_ref[:, lanes], axis=0, keepdims=True))
    for i in range(nx):
        top, total, delta = tops[i], sums[i], deltas[i]
        if i == 0:
            top = jnp.maximum(tops[0], top_w)
            a, b = jnp.exp(tops[0] - top), jnp.exp(top_w - top)
            total = a * sums[0] + b * sum_w
            delta = a * deltas[0] + b * delta_w
        stats[0, i, 0:1, :] = top
        stats[0, i, 1:2, :] = total
        stats[0, i, 2:3, :] = delta
        stats[0, i, 3:8, :] = jnp.zeros((5, BLK), F32)
    for d in range(1, nx):
        start(("st", d), stats.at[0], stats.at[nx - d], st_s.at[d], st_r.at[d], at(0, 0, d))
    o_part = tn(values, s_ref[...].astype(BF16))
    for d in range(1, nx):
        osend[d] = o_part[:, d * BLK:(d + 1) * BLK].astype(BF16)
        start(("o", d), osend.at[d], orecv.at[nx - d], o_s.at[d], o_r.at[d], at(0, 0, d))
    for d in range(1, nx):
        received("st", d)

    logsums, all_deltas = [], []
    for i in range(nx):
        entries = [(stats[p, (i - p) % nx, 0:1, :], stats[p, (i - p) % nx, 1:2, :], stats[p, (i - p) % nx, 2:3, :]) for p in range(nx)]
        top = functools.reduce(jnp.maximum, [e[0] for e in entries])
        logsum = top + jnp.log(sum(e[1] * jnp.exp(e[0] - top) for e in entries))
        logsums.append(logsum)
        all_deltas.append(sum(e[2] * jnp.exp(e[0] - logsum) for e in entries))

    factor_w = jnp.exp(top_w - logsums[0])
    attention = o_part[:, :BLK] * jnp.exp(tops[0] - logsums[0]) + o_w * factor_w
    for d in range(1, nx):
        p = nx - d
        received("o", d)
        attention = attention + orecv[p].astype(F32) * jnp.exp(stats[p, (-p) % nx, 0:1, :] - logsums[0])
    attg[0] = attention.astype(BF16)
    for d in range(1, group):
        start(("att", d), attg.at[0], attg.at[group - d], att_s.at[d], att_r.at[d], member(d))

    weights, grad_scores = [], []
    for i in range(nx):
        lanes = pl.ds(i * BLK, BLK)
        probability = s_ref[:, lanes] * jnp.exp(tops[i] - logsums[i])
        weights.append(probability.astype(BF16))
        grad_scores.append((probability * (dw_ref[:, lanes] - all_deltas[i]) * SCALE).astype(BF16))
    weights = jnp.concatenate(weights, axis=1)
    grad_scores = jnp.concatenate(grad_scores, axis=1)
    gs[:, :, 0] = nn(grad_scores, queries).astype(BF16).reshape(nz, ny, ROWS, HD)
    gs[:, :, 1] = nn(weights, grads).astype(BF16).reshape(nz, ny, ROWS, HD)
    for plane in (1, 0):
        for d in range(1, ny):
            start(("gy", plane, d), gs.at[plane, d], gy.at[plane, ny - d], gy_s.at[plane, d], gy_r.at[plane, d], at(0, d, 0))

    prob_w = p_w * factor_w
    ds_w = (prob_w * (dw_w - all_deltas[0]) * SCALE).astype(BF16)
    gk_w = nn(ds_w, query_own)
    gv_w = nn(prob_w.astype(BF16), grad_own)
    gws[0, 0] = gk_w[:BLK].astype(BF16)
    gws[0, 1] = gv_w[:BLK].astype(BF16)
    gws[1, 0] = gk_w[2 * BLK:].astype(BF16)
    gws[1, 1] = gv_w[2 * BLK:].astype(BF16)
    seam_send(1, grad_ends)

    dq = tn(keys, grad_scores)
    for d in range(1, nx):
        dqs[d] = dq[:, d * BLK:(d + 1) * BLK].astype(BF16)
        start(("dq", d), dqs.at[d], dqr.at[nx - d], dq_s.at[d], dq_r.at[d], at(0, 0, d))
    dq_own = dq[:, :BLK] + tn(key_w, ds_w)

    seam_over(1, grad_ends)
    for load in w_loads:
        load.wait()
    for d in range(1, group):
        for e in range(groups):
            received("w", d, e)
        received("att", d)
    mixed = tn(attg[...].reshape(group * HD, BLK), wg[...].reshape(group * HD, groups * HD))
    for e in range(1, groups):
        msend[e] = mixed[:, e * HD:(e + 1) * HD].astype(BF16)
        start(("mix", e), msend.at[e], mrecv.at[groups - e], mix_s.at[e], mix_r.at[e], other_group(e))
    mixed_own = mixed[:, :HD]

    seam_land(1, grad_ends)
    total = gs[1, 0].astype(F32)
    for d in range(1, ny):
        received("gy", 1, d)
        total = total + gy[1, ny - d].astype(F32)
    gzs[...] = total.astype(BF16)
    start(("gz", 0), gzs, gzr, gz_s.at[0], gz_r.at[0], at(1, 0, 0))

    for d in range(1, nx):
        received("dq", d)
        dq_own = dq_own + dqr[nx - d].astype(F32)
    out_ref[1] = dq_own.T.astype(BF16)

    seam_received(1, grad_ends)
    own_k = gk_w[BLK:2 * BLK] + gwr[0, 0].astype(F32) + gwr[1, 0].astype(F32)
    own_v = gv_w[BLK:2 * BLK] + gwr[0, 1].astype(F32) + gwr[1, 1].astype(F32)
    out_ref[2, ROWS:, :] = own_k[ROWS:].astype(BF16)
    out_ref[3, ROWS:, :] = own_v[ROWS:].astype(BF16)

    total = gs[0, 0].astype(F32)
    for d in range(1, ny):
        received("gy", 0, d)
        total = total + gy[0, ny - d].astype(F32)

    for e in range(1, groups):
        received("mix", e)
        mixed_own = mixed_own + mrecv[groups - e].astype(F32)
    out_ref[0] = mixed_own.astype(BF16)

    received("gz", 0)
    total = total + gzr[...].astype(F32)
    out_ref[2, :ROWS, :] = (own_k[:ROWS] + total[0]).astype(BF16)
    out_ref[3, :ROWS, :] = (own_v[:ROWS] + total[1]).astype(BF16)

    for copy in started.values():
        copy.wait_send()
    seam_sent(0, window_ends)
    seam_sent(1, grad_ends)


def build(mesh, dims, group):
    nz, ny, nx = dims
    heads = mesh.shape["head"]
    groups = heads // group
    chunks = nz * ny

    def shards(queries, key_rows, value_rows, out_weight, strided_index, cotangent):
        width = out_weight.shape[1]
        dma = pltpu.SemaphoreType.DMA
        hbm = pl.BlockSpec(memory_space=pl.ANY)
        vmem = pl.BlockSpec(memory_space=pltpu.VMEM)
        square = lambda n: pltpu.VMEM((n, BLK, HD), BF16)
        pieces = lambda: pltpu.VMEM((nz, ny, 2, ROWS, HD), BF16)
        out = pl.pallas_call(
            functools.partial(kernel, dims, group, heads),
            out_shape=jax.ShapeDtypeStruct((4, BLK, HD), BF16),
            in_specs=[hbm, hbm, hbm, hbm, pl.BlockSpec(memory_space=pltpu.SMEM), hbm],
            out_specs=vmem,
            scratch_shapes=[
                pltpu.VMEM((HD, width), BF16),
                pltpu.VMEM((BLK, width), BF16),
                pltpu.VMEM((3, 2, BLK, HD), BF16),
                pieces(),
                pltpu.VMEM((nx, 2, BLK, HD), BF16),
                pltpu.VMEM((nx, chunks, BLK), F32),
                pltpu.VMEM((group, HD, groups * HD), BF16),
                pltpu.VMEM((nx, nx, 8, BLK), F32),
                square(nx), square(nx),
                square(group),
                square(groups), square(groups),
                square(nx), square(nx),
                pltpu.VMEM((2, 2, BLK, HD), BF16), pltpu.VMEM((2, 2, BLK, HD), BF16),
                pieces(), pieces(),
                pltpu.VMEM((2, ROWS, HD), BF16), pltpu.VMEM((2, ROWS, HD), BF16),
                pltpu.VMEM((chunks * ROWS, nx * BLK), F32),
                pltpu.VMEM((chunks * ROWS, nx * BLK), F32),
                pltpu.VMEM((2, 2, 2, BLK // ny, HD), BF16), pltpu.VMEM((2, 2, 2, BLK // ny, HD), BF16),
                dma((5,)), dma((groups,)),
                dma((1,)), dma((1,)),
                dma((2, ny)), dma((2, ny)),
                dma((2, 2)), dma((2, 2)),
                dma((2, 2, ny)), dma((2, 2)), dma((2, 2)), dma((2, 2)), dma((2, 2)),
                dma((nx,)), dma((nx,)),
                dma((nx,)), dma((nx,)),
                dma((group, groups)), dma((group, groups)),
                dma((nx,)), dma((nx,)),
                dma((nx,)), dma((nx,)),
                dma((nx,)), dma((nx,)),
                dma((2, ny)), dma((2, ny)),
                dma((1,)), dma((1,)),
                dma((group,)), dma((group,)),
                dma((groups,)), dma((groups,)),
            ],
            compiler_params=pltpu.CompilerParams(
                collective_id=0, has_side_effects=True, vmem_limit_bytes=56 * 2 ** 20
            ),
        )(queries, key_rows, value_rows, out_weight, strided_index, cotangent)
        return tuple(out[i] for i in range(4))

    spread = P("seq", "head")
    return jax.shard_map(
        shards,
        mesh=mesh,
        in_specs=(spread, spread, spread, P("head", None), P("seq", None), P("seq", None)),
        out_specs=(spread,) * 4,
        check_vma=False,
    )


def solution(mesh):
    return build(mesh, GRID, GROUP)
```

time: 67.7 us -> 67.9 us (level)
  the two profiles are of different devices: /device:TPU:1 before, /device:TPU:56 now
where the time goes in v2:
time: 67.9 us; the launch traced here: 66.7 us
  Pallas kernels  64.6 us (95%)
  local copies, waits for them, and re-layouts  1.46 us (2%)
    pallas_call x1, Pallas kernels, shards(): pl.pallas_call(functools.partial(kernel, dims, group, heads), out_shape=j...  64.6 us
    squeeze x1, local copies, waits for them, and re-layouts, shards(): return tuple((out[i] for i in range(4)))  1.46 us

profile of v2, /device:TPU:56, one launch (start us, length us, event | category | flops | bytes accessed | tf_op | source)
XLA Modules:
  0.0 66.7 jit_solution(3125876599740131091)
XLA Ops:
  0.6 64.6 %shard_map.93 = bf16[4,128,128]{2,1,0:T(8,128)(2,1)} custom-call(bf16[128,128]{1,0:T(8,128)(2,1)} %q_hbm.1, bf16[128,128]{1,0:T(8,128)(2,1)} %k_hbm.1, bf16[128,128]{1,0:T(8,128)(2,1)} %v_hbm.1, bf16[128,2048]{1,0:T(8,128)(2,1)} %w_hbm.1, s32[1,8]{1,0:T(1,128)} %index_ref.1, bf16[128,2048]{1,0:T(8,128)(2,1)} %ct_hbm.1), custom_call_target="tpu_custom_call" | custom-call | tf_op jit(solution)/shard_map/pallas_call | solution.py:431
  65.2 1.5 %slice_bitcast_fusion = (bf16[128,128]{1,0:T(8,128)(2,1)}, bf16[128,128]{1,0:T(8,128)(2,1)}, bf16[128,128]{1,0:T(8,128)(2,1)}, bf16[128,128]{1,0:T(8,128)(2,1)}) fusion(bf16[4,128,128]{2,1,0:T(8,128)(2,1)} %shard_map.93), kind=kLoop, calls=%fused_computation | loop fusion | bytes 262144 | tf_op jit(solution)/shard_map/squeeze | solution.py:475

commit v3 on v2

--- a/solution.py
+++ b/solution.py
@@ -42,7 +42,6 @@
     st_s, st_r, o_s, o_r, dq_s, dq_r, gy_s, gy_r, gz_s, gz_r, att_s, att_r, mix_s, mix_r,
 ):
     nz, ny, nx = dims
-    count = nz * ny * nx
     groups = heads // group
     seq = lax.axis_index("seq")
     head = lax.axis_index("head")
@@ -58,8 +57,10 @@
     def other_group(e):
         return (seq, (g + e) % groups * group + r)
 
-    following = ((seq + 1) % count, head)
-    preceding = ((seq + count - 1) % count, head)
+    plane = ny * nx
+    place = seq % plane
+    following = (z * plane + (place + 1) % plane, head)
+    preceding = (z * plane + (place + plane - 1) % plane, head)
 
     def send(src, dst, send_sem, recv_sem, device):
         return pltpu.make_async_remote_copy(
@@ -78,41 +79,39 @@
         started[name].wait_recv()
         waited.add(name)
 
-    piece = BLK // ny
+    pieces, piece = 4, BLK // 4
+    is_last = (y == ny - 1) & (x == nx - 1)
     is_first = (y == 0) & (x == 0)
-    is_last = (y == ny - 1) & (x == nx - 1)
-    crossings = (
-        (is_last, x == nx - 1, (y + 1) % ny, following, at(0, -y, 1)),
-        (is_first, x == 0, y, preceding, at(0, ny - 1 - y, nx - 1)),
+    corner = ((y == 0) | (y == ny - 1)) & ((x == 0) | (x == nx - 1))
+    low = (y == 0).astype(jnp.int32) + 2 * (x == 0).astype(jnp.int32)
+    ways = (
+        (is_last, 1, following, low, at(0, -y, -x)),
+        (is_first, -1, preceding, 3 - low, at(0, ny - 1 - y, nx - 1 - x)),
     )
 
-    def seam_copy(kind, way, step, t, src, dst, device):
-        semaphores = (
-            (out_s.at[kind, way, t], in_r.at[kind, way]),
-            (over_s.at[kind, way], over_r.at[kind, way]),
-            (last_s.at[kind, way], win_r.at[kind, way]),
-        )[step]
-        return send(src, dst, *semaphores, device)
-
     def whole(kind, way, src, dst):
-        return send(src, dst, win_s.at[kind, way], win_r.at[kind, way], crossings[way][3])
+        return send(src, dst, win_s.at[kind, way], win_r.at[kind, way], ways[way][2])
 
     def scattered(kind, way, src):
+        step = ways[way][1]
         return [
-            seam_copy(kind, way, 0, t, src.at[:, t * piece:(t + 1) * piece], seam_a.at[kind, way], at(0, t, 0))
-            for t in range(1, ny)
+            send(src.at[:, t * piece:(t + 1) * piece], seam_a.at[kind, way], out_s.at[kind, way, t], in_r.at[kind, way], at(0, step * (t & 1), step * (t >> 1)))
+            for t in range(1, pieces)
         ]
 
     def over(kind, way):
-        return seam_copy(kind, way, 1, 0, seam_a.at[kind, way], seam_b.at[kind, way], at(1, 0, 0))
+        return send(seam_a.at[kind, way], seam_b.at[kind, way], over_s.at[kind, way], over_r.at[kind, way], at(1, 0, 0))
+
+    def over_last(kind, way, dst):
+        return send(seam_a.at[kind, way], dst.at[:, (pieces - 1) * piece:], over_s.at[kind, way], win_r.at[kind, way], at(1, 0, 0))
 
     def landing(kind, way, dst):
-        rows = pl.ds(pl.multiple_of(crossings[way][2] * piece, piece), piece)
-        return seam_copy(kind, way, 2, 0, seam_b.at[kind, way], dst.at[:, rows], crossings[way][4])
+        rows = pl.ds(pl.multiple_of(ways[way][3] * piece, piece), piece)
+        return send(seam_b.at[kind, way], dst.at[:, rows], last_s.at[kind, way], win_r.at[kind, way], ways[way][4])
 
     def seam_send(kind, ends):
         for way, (src, dst) in enumerate(ends):
-            source = crossings[way][0]
+            source = ways[way][0]
 
             @pl.when(source)
             def _():
@@ -125,23 +124,27 @@
                 whole(kind, way, src, dst).start()
 
     def seam_over(kind, ends):
-        for way in range(2):
-            source, column = crossings[way][:2]
-
-            @pl.when(column & jnp.logical_not(source))
-            def _():
-                scattered(kind, way, ends[way][0])[0].wait_recv()
-
-            @pl.when(column)
+        for way, (src, dst) in enumerate(ends):
+            number = ways[way][3]
+
+            @pl.when(corner & (number > 0))
+            def _():
+                scattered(kind, way, src)[0].wait_recv()
+
+            @pl.when(corner & (number < pieces - 1))
             def _():
                 over(kind, way).start()
 
+            @pl.when(corner & (number == pieces - 1))
+            def _():
+                over_last(kind, way, dst).start()
+
     def seam_land(kind, ends):
-        for way in range(2):
-            @pl.when(crossings[way][1])
+        for way, (src, dst) in enumerate(ends):
+            @pl.when(corner & (ways[way][3] < pieces - 1))
             def _():
                 over(kind, way).wait_recv()
-                landing(kind, way, ends[way][1]).start()
+                landing(kind, way, dst).start()
 
     def seam_received(kind, ends):
         for way, (src, dst) in enumerate(ends):
@@ -149,7 +152,7 @@
 
     def seam_sent(kind, ends):
         for way, (src, dst) in enumerate(ends):
-            source, column = crossings[way][:2]
+            source, number = ways[way][0], ways[way][3]
 
             @pl.when(source)
             def _():
@@ -160,9 +163,12 @@
             def _():
                 whole(kind, way, src, dst).wait_send()
 
-            @pl.when(column)
+            @pl.when(corner)
             def _():
                 over(kind, way).wait_send()
+
+            @pl.when(corner & (number < pieces - 1))
+            def _():
                 landing(kind, way, dst).wait_send()
 
     window_ends = ((win.at[1], win.at[0]), (win.at[1], win.at[2]))
@@ -171,29 +177,13 @@
     partners = [at(1, 0, 0)]
     partners += [at(0, d, 0) for d in range(1, ny)]
     partners += [at(0, 0, d) for d in range(1, nx)]
+    partners += [following, preceding]
     partners += [member(d) for d in range(1, group)]
     partners += [other_group(e) for e in range(1, groups)]
     barrier = pltpu.get_barrier_semaphore()
 
-    def greet(device):
+    for device in partners:
         pl.semaphore_signal(barrier, inc=1, device_id=device, device_id_type=MESH)
-
-    for device in partners:
-        greet(device)
-    for way in range(2):
-        @pl.when(jnp.logical_not(crossings[way][0]))
-        def _():
-            greet(crossings[way][3])
-
-        @pl.when(crossings[1 - way][0])
-        def _():
-            for t in range(ny):
-                greet(at(0, t, 1 if way else nx - 1))
-
-    met = len(partners) + sum(
-        jnp.logical_not(source).astype(jnp.int32) + column.astype(jnp.int32)
-        for source, column in (c[:2] for c in crossings)
-    )
 
     loads = [
         pltpu.make_async_copy(k_hbm, win.at[1, 0], local_sem.at[0]),
@@ -215,7 +205,7 @@
     loads[0].wait()
     loads[1].wait()
     kvg[0, 0] = win[1, :, :ROWS, :]
-    pl.semaphore_wait(barrier, met)
+    pl.semaphore_wait(barrier, len(partners))
 
     start(("z", 0), kvg.at[0, 0], kvg.at[1, 0], z_s.at[0], z_r.at[0], at(1, 0, 0))
     for d in range(1, ny):
@@ -230,10 +220,6 @@
     qdo[0, 1] = nt(ct_ref[...], w_ref[...]).astype(BF16)
     for d in range(1, nx):
         start(("qdo", d), qdo.at[0], qdo.at[nx - d], qdo_s.at[d], qdo_r.at[d], at(0, 0, d))
-
-    received("z", 0)
-    for d in range(1, ny):
-        start(("y", 1, d), kvg.at[1, 0], kvg.at[1, ny - d], y_s.at[1, d], y_r.at[1, d], at(0, d, 0))
 
     seam_over(0, window_ends)
     def columns(e, d):
@@ -265,6 +251,11 @@
         dw_ref[rows, :] = nt(values, grads)
 
     strided(0)
+
+    received("z", 0)
+    for d in range(1, ny):
+        start(("y", 1, d), kvg.at[1, 0], kvg.at[1, ny - d], y_s.at[1, d], y_r.at[1, d], at(0, d, 0))
+
 
     seam_land(0, window_ends)
     seam_received(0, window_ends)
@@ -342,9 +333,9 @@
     grad_scores = jnp.concatenate(grad_scores, axis=1)
     gs[:, :, 0] = nn(grad_scores, queries).astype(BF16).reshape(nz, ny, ROWS, HD)
     gs[:, :, 1] = nn(weights, grads).astype(BF16).reshape(nz, ny, ROWS, HD)
-    for plane in (1, 0):
+    for half_index in (1, 0):
         for d in range(1, ny):
-            start(("gy", plane, d), gs.at[plane, d], gy.at[plane, ny - d], gy_s.at[plane, d], gy_r.at[plane, d], at(0, d, 0))
+            start(("gy", half_index, d), gs.at[half_index, d], gy.at[half_index, ny - d], gy_s.at[half_index, d], gy_r.at[half_index, d], at(0, d, 0))
 
     prob_w = p_w * factor_w
     ds_w = (prob_w * (dw_w - all_deltas[0]) * SCALE).astype(BF16)
@@ -451,12 +442,12 @@
                 pltpu.VMEM((2, ROWS, HD), BF16), pltpu.VMEM((2, ROWS, HD), BF16),
                 pltpu.VMEM((chunks * ROWS, nx * BLK), F32),
                 pltpu.VMEM((chunks * ROWS, nx * BLK), F32),
-                pltpu.VMEM((2, 2, 2, BLK // ny, HD), BF16), pltpu.VMEM((2, 2, 2, BLK // ny, HD), BF16),
+                pltpu.VMEM((2, 2, 2, BLK // 4, HD), BF16), pltpu.VMEM((2, 2, 2, BLK // 4, HD), BF16),
                 dma((5,)), dma((groups,)),
                 dma((1,)), dma((1,)),
                 dma((2, ny)), dma((2, ny)),
                 dma((2, 2)), dma((2, 2)),
-                dma((2, 2, ny)), dma((2, 2)), dma((2, 2)), dma((2, 2)), dma((2, 2)),
+                dma((2, 2, 4)), dma((2, 2)), dma((2, 2)), dma((2, 2)), dma((2, 2)),
                 dma((nx,)), dma((nx,)),
                 dma((nx,)), dma((nx,)),
                 dma((group, groups)), dma((group, groups)),

time: 67.9 us -> 67.7 us (level)
  the two profiles are of different devices: /device:TPU:56 before, /device:TPU:64 now
where the time goes in v3:
time: 67.7 us; the launch traced here: 67.5 us
  Pallas kernels  65.4 us (97%)
  local copies, waits for them, and re-layouts  1.46 us (2%)
    pallas_call x1, Pallas kernels, shards(): pl.pallas_call(functools.partial(kernel, dims, group, heads), out_shape=j...  65.4 us
    squeeze x1, local copies, waits for them, and re-layouts, shards(): return tuple((out[i] for i in range(4)))  1.46 us

profile of v3, /device:TPU:64, one launch (start us, length us, event | category | flops | bytes accessed | tf_op | source)
XLA Modules:
  0.0 67.5 jit_solution(10006090463093323612)
XLA Ops:
  0.6 65.4 %shard_map.93 = bf16[4,128,128]{2,1,0:T(8,128)(2,1)} custom-call(bf16[128,128]{1,0:T(8,128)(2,1)} %q_hbm.1, bf16[128,128]{1,0:T(8,128)(2,1)} %k_hbm.1, bf16[128,128]{1,0:T(8,128)(2,1)} %v_hbm.1, bf16[128,2048]{1,0:T(8,128)(2,1)} %w_hbm.1, s32[1,8]{1,0:T(1,128)} %index_ref.1, bf16[128,2048]{1,0:T(8,128)(2,1)} %ct_hbm.1), custom_call_target="tpu_custom_call" | custom-call | tf_op jit(solution)/shard_map/pallas_call | solution.py:422
  66.0 1.5 %slice_bitcast_fusion = (bf16[128,128]{1,0:T(8,128)(2,1)}, bf16[128,128]{1,0:T(8,128)(2,1)}, bf16[128,128]{1,0:T(8,128)(2,1)}, bf16[128,128]{1,0:T(8,128)(2,1)}) fusion(bf16[4,128,128]{2,1,0:T(8,128)(2,1)} %shard_map.93), kind=kLoop, calls=%fused_computation | loop fusion | bytes 262144 | tf_op jit(solution)/shard_map/squeeze | solution.py:466

commit v4 on v3

--- a/solution.py
+++ b/solution.py
@@ -36,9 +36,9 @@
     q_hbm, k_hbm, v_hbm, w_hbm, index_ref, ct_hbm,
     out_ref,
     w_ref, ct_ref, win, kvg, qdo, bias, wg, stats, osend, orecv, attg, msend, mrecv,
-    dqs, dqr, gws, gwr, gs, gy, gzs, gzr, s_ref, dw_ref, seam_a, seam_b,
+    dqs, dqr, near, own_rows, near_rows, relay_rows, gs, gy, gzs, gzr, s_ref, dw_ref, seam_a, seam_b,
     local_sem, w_local_sem,
-    z_s, z_r, y_s, y_r, win_s, win_r, out_s, in_r, over_s, over_r, last_s, qdo_s, qdo_r, bias_s, bias_r, w_s, w_r,
+    z_s, z_r, y_s, y_r, win_s, win_r, out_s, in_r, over_s, over_r, last_s, row_s, row_r, relay_s, relay_r, qdo_s, qdo_r, bias_s, bias_r, w_s, w_r,
     st_s, st_r, o_s, o_r, dq_s, dq_r, gy_s, gy_r, gz_s, gz_r, att_s, att_r, mix_s, mix_r,
 ):
     nz, ny, nx = dims
@@ -171,8 +171,21 @@
             def _():
                 landing(kind, way, dst).wait_send()
 
+    def row_copy(way, source):
+        to, arrived = (relay_rows.at[way], relay_r.at[way]) if source else (near_rows.at[way], row_r.at[way])
+        return send(own_rows, to, row_s.at[way], arrived, ways[way][2])
+
+    def row_relay(way):
+        return send(relay_rows.at[way], near_rows.at[way], relay_s.at[way], row_r.at[way], at(1, 0, 0))
+
+    def either(way, action):
+        for source in (True, False):
+            @pl.when(ways[way][0] == source)
+            def _():
+                action(row_copy(way, source))
+
     window_ends = ((win.at[1], win.at[0]), (win.at[1], win.at[2]))
-    grad_ends = ((gws.at[1], gwr.at[1]), (gws.at[0], gwr.at[0]))
+    query_ends = ((qdo.at[0], near.at[0]), (qdo.at[0], near.at[1]))
 
     partners = [at(1, 0, 0)]
     partners += [at(0, d, 0) for d in range(1, ny)]
@@ -205,23 +218,47 @@
     loads[0].wait()
     loads[1].wait()
     kvg[0, 0] = win[1, :, :ROWS, :]
-    pl.semaphore_wait(barrier, len(partners))
-
-    start(("z", 0), kvg.at[0, 0], kvg.at[1, 0], z_s.at[0], z_r.at[0], at(1, 0, 0))
-    for d in range(1, ny):
-        start(("y", 0, d), kvg.at[0, 0], kvg.at[0, ny - d], y_s.at[0, d], y_r.at[0, d], at(0, d, 0))
-    seam_send(0, window_ends)
-    for d in range(1, nx):
-        start(("bias", d), bias.at[0], bias.at[nx - d], bias_s.at[d], bias_r.at[d], at(0, 0, d))
-
     loads[2].wait()
     loads[3].wait()
     loads[4].wait()
     qdo[0, 1] = nt(ct_ref[...], w_ref[...]).astype(BF16)
+    pl.semaphore_wait(barrier, len(partners))
+
+    seam_send(0, window_ends)
+    start(("z", 0), kvg.at[0, 0], kvg.at[1, 0], z_s.at[0], z_r.at[0], at(1, 0, 0))
+    for d in range(1, ny):
+        start(("y", 0, d), kvg.at[0, 0], kvg.at[0, ny - d], y_s.at[0, d], y_r.at[0, d], at(0, d, 0))
+    for d in range(1, nx):
+        start(("bias", d), bias.at[0], bias.at[nx - d], bias_s.at[d], bias_r.at[d], at(0, 0, d))
+
     for d in range(1, nx):
         start(("qdo", d), qdo.at[0], qdo.at[nx - d], qdo_s.at[d], qdo_r.at[d], at(0, 0, d))
 
+    seam_send(1, query_ends)
     seam_over(0, window_ends)
+    for d in range(1, nx):
+        received("bias", d)
+        received("qdo", d)
+    queries = qdo[:, 0].reshape(nx * BLK, HD)
+    grads = qdo[:, 1].reshape(nx * BLK, HD)
+    half = ny * ROWS
+
+    def strided(plane):
+        for d in range(1, ny):
+            received("y", plane, d)
+        rows = pl.ds(plane * half, half)
+        keys = kvg[plane, :, 0].reshape(half, HD)
+        values = kvg[plane, :, 1].reshape(half, HD)
+        s_ref[rows, :] = nt(keys, queries)
+        dw_ref[rows, :] = nt(values, grads)
+
+    strided(0)
+
+    received("z", 0)
+    for d in range(1, ny):
+        start(("y", 1, d), kvg.at[1, 0], kvg.at[1, ny - d], y_s.at[1, d], y_r.at[1, d], at(0, d, 0))
+
+
     def columns(e, d):
         return pl.ds(pl.multiple_of(((g + e) % groups * group + (r + d) % group) * HD, HD), HD)
 
@@ -233,29 +270,6 @@
         w_loads.append(load)
         for d in range(1, group):
             start(("w", d, e), w_hbm.at[:, columns(e, d)], wg.at[group - d, :, to], w_s.at[d, e], w_r.at[d, e], member(d))
-
-    for d in range(1, nx):
-        received("bias", d)
-        received("qdo", d)
-    queries = qdo[:, 0].reshape(nx * BLK, HD)
-    grads = qdo[:, 1].reshape(nx * BLK, HD)
-    half = ny * ROWS
-
-    def strided(plane):
-        for d in range(1, ny):
-            received("y", plane, d)
-        rows = pl.ds(plane * half, half)
-        keys = kvg[plane, :, 0].reshape(half, HD)
-        values = kvg[plane, :, 1].reshape(half, HD)
-        s_ref[rows, :] = nt(keys, queries)
-        dw_ref[rows, :] = nt(values, grads)
-
-    strided(0)
-
-    received("z", 0)
-    for d in range(1, ny):
-        start(("y", 1, d), kvg.at[1, 0], kvg.at[1, ny - d], y_s.at[1, d], y_r.at[1, d], at(0, d, 0))
-
 
     seam_land(0, window_ends)
     seam_received(0, window_ends)
@@ -270,6 +284,7 @@
     delta_w = jnp.sum(p_w * dw_w, axis=0, keepdims=True)
     o_w = tn(value_w, p_w.astype(BF16))
 
+    seam_over(1, query_ends)
     strided(1)
     chunks = nz * ny
     keys = kvg[:, :, 0].reshape(chunks * ROWS, HD)
@@ -313,15 +328,11 @@
         logsums.append(logsum)
         all_deltas.append(sum(e[2] * jnp.exp(e[0] - logsum) for e in entries))
 
-    factor_w = jnp.exp(top_w - logsums[0])
-    attention = o_part[:, :BLK] * jnp.exp(tops[0] - logsums[0]) + o_w * factor_w
-    for d in range(1, nx):
-        p = nx - d
-        received("o", d)
-        attention = attention + orecv[p].astype(F32) * jnp.exp(stats[p, (-p) % nx, 0:1, :] - logsums[0])
-    attg[0] = attention.astype(BF16)
-    for d in range(1, group):
-        start(("att", d), attg.at[0], attg.at[group - d], att_s.at[d], att_r.at[d], member(d))
+    own_rows[0:1, :] = logsums[0]
+    own_rows[1:2, :] = all_deltas[0]
+    own_rows[2:8, :] = jnp.zeros((6, BLK), F32)
+    for way in range(2):
+        either(way, lambda copy: copy.start())
 
     weights, grad_scores = [], []
     for i in range(nx):
@@ -333,19 +344,34 @@
     grad_scores = jnp.concatenate(grad_scores, axis=1)
     gs[:, :, 0] = nn(grad_scores, queries).astype(BF16).reshape(nz, ny, ROWS, HD)
     gs[:, :, 1] = nn(weights, grads).astype(BF16).reshape(nz, ny, ROWS, HD)
-    for half_index in (1, 0):
-        for d in range(1, ny):
-            start(("gy", half_index, d), gs.at[half_index, d], gy.at[half_index, ny - d], gy_s.at[half_index, d], gy_r.at[half_index, d], at(0, d, 0))
-
+    for d in range(1, ny):
+        start(("gy", 1, d), gs.at[1, d], gy.at[1, ny - d], gy_s.at[1, d], gy_r.at[1, d], at(0, d, 0))
+
+    factor_w = jnp.exp(top_w - logsums[0])
     prob_w = p_w * factor_w
     ds_w = (prob_w * (dw_w - all_deltas[0]) * SCALE).astype(BF16)
-    gk_w = nn(ds_w, query_own)
-    gv_w = nn(prob_w.astype(BF16), grad_own)
-    gws[0, 0] = gk_w[:BLK].astype(BF16)
-    gws[0, 1] = gv_w[:BLK].astype(BF16)
-    gws[1, 0] = gk_w[2 * BLK:].astype(BF16)
-    gws[1, 1] = gv_w[2 * BLK:].astype(BF16)
-    seam_send(1, grad_ends)
+    own_k = nn(ds_w[BLK:2 * BLK], query_own)
+    own_v = nn(prob_w[BLK:2 * BLK].astype(BF16), grad_own)
+
+    attention = o_part[:, :BLK] * jnp.exp(tops[0] - logsums[0]) + o_w * factor_w
+    for d in range(1, nx):
+        p = nx - d
+        received("o", d)
+        attention = attention + orecv[p].astype(F32) * jnp.exp(stats[p, (-p) % nx, 0:1, :] - logsums[0])
+    attg[0] = attention.astype(BF16)
+    for d in range(1, group):
+        start(("att", d), attg.at[0], attg.at[group - d], att_s.at[d], att_r.at[d], member(d))
+
+    for way in range(2):
+        @pl.when(ways[1 - way][0])
+        def _():
+            row_copy(way, True).wait_recv()
+            row_relay(way).start()
+
+    for d in range(1, ny):
+        start(("gy", 0, d), gs.at[0, d], gy.at[0, ny - d], gy_s.at[0, d], gy_r.at[0, d], at(0, d, 0))
+
+    seam_land(1, query_ends)
 
     dq = tn(keys, grad_scores)
     for d in range(1, nx):
@@ -353,7 +379,6 @@
         start(("dq", d), dqs.at[d], dqr.at[nx - d], dq_s.at[d], dq_r.at[d], at(0, 0, d))
     dq_own = dq[:, :BLK] + tn(key_w, ds_w)
 
-    seam_over(1, grad_ends)
     for load in w_loads:
         load.wait()
     for d in range(1, group):
@@ -366,7 +391,6 @@
         start(("mix", e), msend.at[e], mrecv.at[groups - e], mix_s.at[e], mix_r.at[e], other_group(e))
     mixed_own = mixed[:, :HD]
 
-    seam_land(1, grad_ends)
     total = gs[1, 0].astype(F32)
     for d in range(1, ny):
         received("gy", 1, d)
@@ -379,9 +403,16 @@
         dq_own = dq_own + dqr[nx - d].astype(F32)
     out_ref[1] = dq_own.T.astype(BF16)
 
-    seam_received(1, grad_ends)
-    own_k = gk_w[BLK:2 * BLK] + gwr[0, 0].astype(F32) + gwr[1, 0].astype(F32)
-    own_v = gv_w[BLK:2 * BLK] + gwr[0, 1].astype(F32) + gwr[1, 1].astype(F32)
+    seam_received(1, query_ends)
+    for way in range(2):
+        query_near, grad_near = near[way, 0], near[way, 1]
+        score = nt(win[1, 0], query_near) * SCALE
+        dw = nt(win[1, 1], grad_near)
+        row_copy(way, False).wait_recv()
+        probability = jnp.exp(score - near_rows[way, 0:1, :])
+        ds = (probability * (dw - near_rows[way, 1:2, :]) * SCALE).astype(BF16)
+        own_k = own_k + nn(ds, query_near)
+        own_v = own_v + nn(probability.astype(BF16), grad_near)
     out_ref[2, ROWS:, :] = own_k[ROWS:].astype(BF16)
     out_ref[3, ROWS:, :] = own_v[ROWS:].astype(BF16)
 
@@ -403,7 +434,13 @@
     for copy in started.values():
         copy.wait_send()
     seam_sent(0, window_ends)
-    seam_sent(1, grad_ends)
+    seam_sent(1, query_ends)
+    for way in range(2):
+        either(way, lambda copy: copy.wait_send())
+
+        @pl.when(ways[1 - way][0])
+        def _():
+            row_relay(way).wait_send()
 
 
 def build(mesh, dims, group):
@@ -437,7 +474,7 @@
                 square(group),
                 square(groups), square(groups),
                 square(nx), square(nx),
-                pltpu.VMEM((2, 2, BLK, HD), BF16), pltpu.VMEM((2, 2, BLK, HD), BF16),
+                pltpu.VMEM((2, 2, BLK, HD), BF16), pltpu.VMEM((8, BLK), F32), pltpu.VMEM((2, 8, BLK), F32), pltpu.VMEM((2, 8, BLK), F32),
                 pieces(), pieces(),
                 pltpu.VMEM((2, ROWS, HD), BF16), pltpu.VMEM((2, ROWS, HD), BF16),
                 pltpu.VMEM((chunks * ROWS, nx * BLK), F32),
@@ -448,6 +485,7 @@
                 dma((2, ny)), dma((2, ny)),
                 dma((2, 2)), dma((2, 2)),
                 dma((2, 2, 4)), dma((2, 2)), dma((2, 2)), dma((2, 2)), dma((2, 2)),
+                dma((2,)), dma((2,)), dma((2,)), dma((2,)),
                 dma((nx,)), dma((nx,)),
                 dma((nx,)), dma((nx,)),
                 dma((group, groups)), dma((group, groups)),

time: 67.7 us -> 61.8 us (0.913)
  the two profiles are of different devices: /device:TPU:64 before, /device:TPU:56 now
where the time goes in v4:
time: 61.8 us; the launch traced here: 60.8 us
  Pallas kernels  58.7 us (95%)
  local copies, waits for them, and re-layouts  1.46 us (2%)
  between operations  0.64 us (1%)
    pallas_call x1, Pallas kernels, shards(): pl.pallas_call(functools.partial(kernel, dims, group, heads), out_shape=j...  58.7 us
    squeeze x1, local copies, waits for them, and re-layouts, shards(): return tuple((out[i] for i in range(4)))  1.46 us

profile of v4, /device:TPU:56, one launch (start us, length us, event | category | flops | bytes accessed | tf_op | source)
XLA Modules:
  0.0 60.8 jit_solution(5204130018919561826)
XLA Ops:
  0.6 58.7 %shard_map.93 = bf16[4,128,128]{2,1,0:T(8,128)(2,1)} custom-call(bf16[128,128]{1,0:T(8,128)(2,1)} %q_hbm.1, bf16[128,128]{1,0:T(8,128)(2,1)} %k_hbm.1, bf16[128,128]{1,0:T(8,128)(2,1)} %v_hbm.1, bf16[128,2048]{1,0:T(8,128)(2,1)} %w_hbm.1, s32[1,8]{1,0:T(1,128)} %index_ref.1, bf16[128,2048]{1,0:T(8,128)(2,1)} %ct_hbm.1), custom_call_target="tpu_custom_call" | custom-call | tf_op jit(solution)/shard_map/pallas_call | solution.py:459
  59.3 1.5 %slice_bitcast_fusion = (bf16[128,128]{1,0:T(8,128)(2,1)}, bf16[128,128]{1,0:T(8,128)(2,1)}, bf16[128,128]{1,0:T(8,128)(2,1)}, bf16[128,128]{1,0:T(8,128)(2,1)}) fusion(bf16[4,128,128]{2,1,0:T(8,128)(2,1)} %shard_map.93), kind=kLoop, calls=%fused_computation | loop fusion | bytes 262144 | tf_op jit(solution)/shard_map/squeeze | solution.py:504

commit v5 on v4

--- a/solution.py
+++ b/solution.py
@@ -109,9 +109,13 @@
         rows = pl.ds(pl.multiple_of(ways[way][3] * piece, piece), piece)
         return send(seam_b.at[kind, way], dst.at[:, rows], last_s.at[kind, way], win_r.at[kind, way], ways[way][4])
 
+    def outer(kind, way):
+        return (x == (0 if way else nx - 1)) | (kind == 0)
+
     def seam_send(kind, ends):
         for way, (src, dst) in enumerate(ends):
             source = ways[way][0]
+            outside = outer(kind, way)
 
             @pl.when(source)
             def _():
@@ -119,7 +123,7 @@
                     copy.start()
                 seam_a[kind, way] = src[:, :piece]
 
-            @pl.when(jnp.logical_not(source))
+            @pl.when(jnp.logical_not(source) & outside)
             def _():
                 whole(kind, way, src, dst).start()
 
@@ -148,7 +152,16 @@
 
     def seam_received(kind, ends):
         for way, (src, dst) in enumerate(ends):
-            whole(kind, way, src, dst).wait_recv()
+            outside = outer(kind, 1 - way)
+
+            @pl.when(outside)
+            def _():
+                whole(kind, way, src, dst).wait_recv()
+
+            if kind == 1:
+                @pl.when(jnp.logical_not(outside))
+                def _():
+                    dst[...] = qdo[1 if way else nx - 1]
 
     def seam_sent(kind, ends):
         for way, (src, dst) in enumerate(ends):
@@ -159,7 +172,7 @@
                 for copy in scattered(kind, way, src):
                     copy.wait_send()
 
-            @pl.when(jnp.logical_not(source))
+            @pl.when(jnp.logical_not(source) & outer(kind, way))
             def _():
                 whole(kind, way, src, dst).wait_send()
 
@@ -224,8 +237,8 @@
     qdo[0, 1] = nt(ct_ref[...], w_ref[...]).astype(BF16)
     pl.semaphore_wait(barrier, len(partners))
 
+    start(("z", 0), kvg.at[0, 0], kvg.at[1, 0], z_s.at[0], z_r.at[0], at(1, 0, 0))
     seam_send(0, window_ends)
-    start(("z", 0), kvg.at[0, 0], kvg.at[1, 0], z_s.at[0], z_r.at[0], at(1, 0, 0))
     for d in range(1, ny):
         start(("y", 0, d), kvg.at[0, 0], kvg.at[0, ny - d], y_s.at[0, d], y_r.at[0, d], at(0, d, 0))
     for d in range(1, nx):
@@ -234,8 +247,13 @@
     for d in range(1, nx):
         start(("qdo", d), qdo.at[0], qdo.at[nx - d], qdo_s.at[d], qdo_r.at[d], at(0, 0, d))
 
+    seam_over(0, window_ends)
+    received("z", 0)
+    for d in range(1, ny):
+        start(("y", 1, d), kvg.at[1, 0], kvg.at[1, ny - d], y_s.at[1, d], y_r.at[1, d], at(0, d, 0))
+
+
     seam_send(1, query_ends)
-    seam_over(0, window_ends)
     for d in range(1, nx):
         received("bias", d)
         received("qdo", d)
@@ -253,11 +271,6 @@
         dw_ref[rows, :] = nt(values, grads)
 
     strided(0)
-
-    received("z", 0)
-    for d in range(1, ny):
-        start(("y", 1, d), kvg.at[1, 0], kvg.at[1, ny - d], y_s.at[1, d], y_r.at[1, d], at(0, d, 0))
-
 
     def columns(e, d):
         return pl.ds(pl.multiple_of(((g + e) % groups * group + (r + d) % group) * HD, HD), HD)
@@ -342,8 +355,12 @@
         grad_scores.append((probability * (dw_ref[:, lanes] - all_deltas[i]) * SCALE).astype(BF16))
     weights = jnp.concatenate(weights, axis=1)
     grad_scores = jnp.concatenate(grad_scores, axis=1)
-    gs[:, :, 0] = nn(grad_scores, queries).astype(BF16).reshape(nz, ny, ROWS, HD)
-    gs[:, :, 1] = nn(weights, grads).astype(BF16).reshape(nz, ny, ROWS, HD)
+    def collect(plane):
+        rows = slice(plane * half, (plane + 1) * half)
+        gs[plane, :, 0] = nn(grad_scores[rows], queries).astype(BF16).reshape(ny, ROWS, HD)
+        gs[plane, :, 1] = nn(weights[rows], grads).astype(BF16).reshape(ny, ROWS, HD)
+
+    collect(1)
     for d in range(1, ny):
         start(("gy", 1, d), gs.at[1, d], gy.at[1, ny - d], gy_s.at[1, d], gy_r.at[1, d], at(0, d, 0))
 
@@ -368,6 +385,7 @@
             row_copy(way, True).wait_recv()
             row_relay(way).start()
 
+    collect(0)
     for d in range(1, ny):
         start(("gy", 0, d), gs.at[0, d], gy.at[0, ny - d], gy_s.at[0, d], gy_r.at[0, d], at(0, d, 0))
 

time: 61.8 us -> 61.1 us (0.989); the launches traced: 60.8 us -> 60.9 us
  no operation moved by 1% of the time
where the time goes in v5:
time: 61.1 us; the launch traced here: 60.9 us
  Pallas kernels  58.8 us (96%)
  local copies, waits for them, and re-layouts  1.46 us (2%)
  between operations  0.64 us (1%)
    pallas_call x1, Pallas kernels, shards(): pl.pallas_call(functools.partial(kernel, dims, group, heads), out_shape=j...  58.8 us
    squeeze x1, local copies, waits for them, and re-layouts, shards(): return tuple((out[i] for i in range(4)))  1.46 us

profile of v5, /device:TPU:56, one launch (start us, length us, event | category | flops | bytes accessed | tf_op | source)
XLA Modules:
  0.0 60.9 jit_solution(12374144398707819048)
XLA Ops:
  0.6 58.8 %shard_map.93 = bf16[4,128,128]{2,1,0:T(8,128)(2,1)} custom-call(bf16[128,128]{1,0:T(8,128)(2,1)} %q_hbm.1, bf16[128,128]{1,0:T(8,128)(2,1)} %k_hbm.1, bf16[128,128]{1,0:T(8,128)(2,1)} %v_hbm.1, bf16[128,2048]{1,0:T(8,128)(2,1)} %w_hbm.1, s32[1,8]{1,0:T(1,128)} %index_ref.1, bf16[128,2048]{1,0:T(8,128)(2,1)} %ct_hbm.1), custom_call_target="tpu_custom_call" | custom-call | tf_op jit(solution)/shard_map/pallas_call | solution.py:477
  59.4 1.5 %slice_bitcast_fusion = (bf16[128,128]{1,0:T(8,128)(2,1)}, bf16[128,128]{1,0:T(8,128)(2,1)}, bf16[128,128]{1,0:T(8,128)(2,1)}, bf16[128,128]{1,0:T(8,128)(2,1)}) fusion(bf16[4,128,128]{2,1,0:T(8,128)(2,1)} %shard_map.93), kind=kLoop, calls=%fused_computation | loop fusion | bytes 262144 | tf_op jit(solution)/shard_map/squeeze | solution.py:522

commit v6 on v5

--- a/solution.py
+++ b/solution.py
@@ -17,6 +17,10 @@
 BF16 = jnp.bfloat16
 SCALE = HD ** -0.5
 EXCLUDED = -1e30
+
+
+def far(size):
+    return sorted(range(1, size), key=lambda d: -min(d, size - d))
 
 
 def nt(a, b):
@@ -239,17 +243,17 @@
 
     start(("z", 0), kvg.at[0, 0], kvg.at[1, 0], z_s.at[0], z_r.at[0], at(1, 0, 0))
     seam_send(0, window_ends)
-    for d in range(1, ny):
+    for d in far(ny):
         start(("y", 0, d), kvg.at[0, 0], kvg.at[0, ny - d], y_s.at[0, d], y_r.at[0, d], at(0, d, 0))
-    for d in range(1, nx):
+    for d in far(nx):
         start(("bias", d), bias.at[0], bias.at[nx - d], bias_s.at[d], bias_r.at[d], at(0, 0, d))
 
-    for d in range(1, nx):
+    for d in far(nx):
         start(("qdo", d), qdo.at[0], qdo.at[nx - d], qdo_s.at[d], qdo_r.at[d], at(0, 0, d))
 
     seam_over(0, window_ends)
     received("z", 0)
-    for d in range(1, ny):
+    for d in far(ny):
         start(("y", 1, d), kvg.at[1, 0], kvg.at[1, ny - d], y_s.at[1, d], y_r.at[1, d], at(0, d, 0))
 
 
@@ -324,10 +328,10 @@
         stats[0, i, 1:2, :] = total
         stats[0, i, 2:3, :] = delta
         stats[0, i, 3:8, :] = jnp.zeros((5, BLK), F32)
-    for d in range(1, nx):
+    for d in far(nx):
         start(("st", d), stats.at[0], stats.at[nx - d], st_s.at[d], st_r.at[d], at(0, 0, d))
     o_part = tn(values, s_ref[...].astype(BF16))
-    for d in range(1, nx):
+    for d in far(nx):
         osend[d] = o_part[:, d * BLK:(d + 1) * BLK].astype(BF16)
         start(("o", d), osend.at[d], orecv.at[nx - d], o_s.at[d], o_r.at[d], at(0, 0, d))
     for d in range(1, nx):
@@ -361,7 +365,7 @@
         gs[plane, :, 1] = nn(weights[rows], grads).astype(BF16).reshape(ny, ROWS, HD)
 
     collect(1)
-    for d in range(1, ny):
+    for d in far(ny):
         start(("gy", 1, d), gs.at[1, d], gy.at[1, ny - d], gy_s.at[1, d], gy_r.at[1, d], at(0, d, 0))
 
     factor_w = jnp.exp(top_w - logsums[0])
@@ -386,13 +390,13 @@
             row_relay(way).start()
 
     collect(0)
-    for d in range(1, ny):
+    for d in far(ny):
         start(("gy", 0, d), gs.at[0, d], gy.at[0, ny - d], gy_s.at[0, d], gy_r.at[0, d], at(0, d, 0))
 
     seam_land(1, query_ends)
 
     dq = tn(keys, grad_scores)
-    for d in range(1, nx):
+    for d in far(nx):
         dqs[d] = dq[:, d * BLK:(d + 1) * BLK].astype(BF16)
         start(("dq", d), dqs.at[d], dqr.at[nx - d], dq_s.at[d], dq_r.at[d], at(0, 0, d))
     dq_own = dq[:, :BLK] + tn(key_w, ds_w)

time: 61.1 us -> 61.4 us (level)
  no operation moved by 1% of the time
where the time goes in v6:
time: 61.4 us; the launch traced here: 60.8 us
  Pallas kernels  58.7 us (96%)
  local copies, waits for them, and re-layouts  1.46 us (2%)
  between operations  0.64 us (1%)
    pallas_call x1, Pallas kernels, shards(): pl.pallas_call(functools.partial(kernel, dims, group, heads), out_shape=j...  58.7 us
    squeeze x1, local copies, waits for them, and re-layouts, shards(): return tuple((out[i] for i in range(4)))  1.46 us

profile of v6, /device:TPU:56, one launch (start us, length us, event | category | flops | bytes accessed | tf_op | source)
XLA Modules:
  0.0 60.8 jit_solution(9371824245559120776)
XLA Ops:
  0.6 58.7 %shard_map.93 = bf16[4,128,128]{2,1,0:T(8,128)(2,1)} custom-call(bf16[128,128]{1,0:T(8,128)(2,1)} %q_hbm.1, bf16[128,128]{1,0:T(8,128)(2,1)} %k_hbm.1, bf16[128,128]{1,0:T(8,128)(2,1)} %v_hbm.1, bf16[128,2048]{1,0:T(8,128)(2,1)} %w_hbm.1, s32[1,8]{1,0:T(1,128)} %index_ref.1, bf16[128,2048]{1,0:T(8,128)(2,1)} %ct_hbm.1), custom_call_target="tpu_custom_call" | custom-call | tf_op jit(solution)/shard_map/pallas_call | solution.py:481
  59.3 1.5 %slice_bitcast_fusion = (bf16[128,128]{1,0:T(8,128)(2,1)}, bf16[128,128]{1,0:T(8,128)(2,1)}, bf16[128,128]{1,0:T(8,128)(2,1)}, bf16[128,128]{1,0:T(8,128)(2,1)}) fusion(bf16[4,128,128]{2,1,0:T(8,128)(2,1)} %shard_map.93), kind=kLoop, calls=%fused_computation | loop fusion | bytes 262144 | tf_op jit(solution)/shard_map/squeeze | solution.py:526
